TPU v7x, 32 devices: a whole 2x2x4 slice. The times are simulated.
32 devices in a mesh: grp: 4 (over x, core), ep: 4 (over z), sq: 2 (over y).
Axes of the slice: x: 2, y: 2, z: 4, core: 2. Of those that a mesh axis runs over, the one named last changes fastest.
Arguments:
- queries: bfloat16 [8192, 2048], P(('grp', 'ep', 'sq')), may hold values from -32 to 32
- keys: bfloat16 [8192, 512], P(('grp', 'ep', 'sq')), may hold values from -32 to 32
- values: bfloat16 [8192, 512], P(('grp', 'ep', 'sq')), may hold values from -6 to 6
- norm_gain: float32 [2048], replicated, may hold values from 0.1 to 1.9
- expert_ids: int32 [8192, 2], P(('grp', 'ep', 'sq')), may hold values from 0 to 3, all different within a row; in each aligned block of 256 rows (0 to 255, 256 to 511, ...) at most 192 rows name the same one
- gate_values: float32 [8192, 2], P(('grp', 'ep', 'sq')), may hold values from 0.1 to 1
- hidden_grad: bfloat16 [8192, 1024], P(('grp', 'ep', 'sq')), may hold values from -0.59765625 to 0.59765625
- gate_weight: bfloat16 [4, 2048, 1024], P('ep', None, 'sq'), may hold values from -0.125 to 0.125
- up_weight: bfloat16 [4, 2048, 1024], P('ep', None, 'sq'), may hold values from -0.125 to 0.125
Outputs:
- gate_grad: float32 [4, 2048, 1024], P('ep', 'grp', 'sq')
Inputs may be any that keep to these rules, and one draw needn't show every extreme that they name: `expert_ids`: each token names 2 different experts; within the 256 tokens of one device no expert is named more than 192 times.
All inputs are finite; a program needn't handle non-finite values.
Results may differ from a plain program's by a relative error of at most 0.0085.
Values may be sent and summed in bfloat16 or wider, within the bound.
A program may use at most 64 MiB of HBM per device.

v0:
```python
import math

import jax
import jax.numpy as jnp
from jax import lax
from jax.sharding import PartitionSpec as P

HEAD_DIM = 128
LENGTH = 512


epsilon = 1e-05
masked_score = -1e30


def gate_term(inputs, cotangent, weight_gate, weight_up):
    pre_gate = jnp.dot(inputs, weight_gate, preferred_element_type=jnp.float32)
    pre_up = jnp.dot(inputs, weight_up, preferred_element_type=jnp.float32)
    sigmoid_gate = jax.nn.sigmoid(pre_gate)
    slope = sigmoid_gate * (1.0 + pre_gate * (1.0 - sigmoid_gate))
    delta_gate = (cotangent.astype(jnp.float32) * pre_up * slope).astype(jnp.bfloat16)
    return lax.dot_general(
        inputs, delta_gate, (((0,), (0,)), ((), ())), preferred_element_type=jnp.float32
    )


def body(
    queries, keys, values, norm_gain, expert_ids, gate_values, hidden_grad, gate_weight, up_weight
):
    rows_here, model_width = queries.shape
    kv_width = keys.shape[1]
    kv_heads = kv_width // HEAD_DIM
    group_size = model_width // kv_width
    score_scale = 1.0 / math.sqrt(HEAD_DIM)
    shard_index = lax.axis_index("sq")
    query_positions = shard_index * rows_here + jnp.arange(rows_here, dtype=jnp.int32)
    query_sequence = query_positions // LENGTH
    query_heads = queries.reshape(rows_here, kv_heads, group_size, HEAD_DIM)
    running_max = jnp.full((rows_here, kv_heads, group_size), masked_score, jnp.float32)
    key_rows = lax.all_gather(keys, "sq", axis=0, tiled=True)
    value_rows = lax.all_gather(values, "sq", axis=0, tiled=True)
    key_count = key_rows.shape[0]
    key_heads = key_rows.reshape(key_count, kv_heads, HEAD_DIM)
    value_heads = value_rows.reshape(key_count, kv_heads, HEAD_DIM)
    scores = (
        jnp.einsum("tkgd,rkd->tkgr", query_heads, key_heads, preferred_element_type=jnp.float32)
        * score_scale
    )
    key_positions = jnp.arange(key_count, dtype=jnp.int32)
    causal = key_positions[None, :] <= query_positions[:, None]
    same_sequence = (key_positions // LENGTH)[None, :] == query_sequence[:, None]
    allowed = (causal & same_sequence)[:, None, None, :]
    scores = jnp.where(allowed, scores, masked_score)
    updated_max = jnp.maximum(running_max, jnp.max(scores, axis=-1))
    exponent_terms = jnp.where(allowed, jnp.exp(scores - updated_max[..., None]), 0.0)
    running_sum = jnp.sum(exponent_terms, axis=-1)
    running_out = jnp.einsum(
        "tkgr,rkd->tkgd",
        exponent_terms.astype(jnp.bfloat16),
        value_heads,
        preferred_element_type=jnp.float32,
    )
    attended = (running_out / running_sum[..., None]).reshape(rows_here, model_width)
    mean_square = jnp.mean(attended * attended, axis=-1, keepdims=True)
    normed = (attended * lax.rsqrt(mean_square + epsilon) * norm_gain).astype(jnp.bfloat16)
    top_count = expert_ids.shape[1]
    experts = lax.axis_size("ep")
    capacity = rows_here * top_count // experts * 3 // 2
    hidden_width = hidden_grad.shape[1]
    flat_ids = expert_ids.reshape(-1)
    one_hot = (flat_ids[:, None] == jnp.arange(experts, dtype=jnp.int32)[None, :]).astype(jnp.int32)
    slot_rank = jnp.sum(jnp.cumsum(one_hot, axis=0) * one_hot, axis=1) - 1
    slot_target = flat_ids * capacity + slot_rank
    routed_inputs = jnp.repeat(normed, top_count, axis=0)
    routed_grad = (
        gate_values.reshape(-1, 1) * jnp.repeat(hidden_grad, top_count, axis=0).astype(jnp.float32)
    ).astype(jnp.bfloat16)
    send_inputs = (
        jnp.zeros((experts * capacity, model_width), jnp.bfloat16)
        .at[slot_target]
        .set(routed_inputs)
    )
    send_grad = (
        jnp.zeros((experts * capacity, hidden_width), jnp.bfloat16).at[slot_target].set(routed_grad)
    )
    send_inputs = send_inputs.reshape(experts, capacity, model_width)
    send_grad = send_grad.reshape(experts, capacity, hidden_width)
    got_inputs, got_grad = (
        lax.all_to_all(send_inputs, "ep", split_axis=0, concat_axis=0, tiled=True),
        lax.all_to_all(send_grad, "ep", split_axis=0, concat_axis=0, tiled=True),
    )
    expert_inputs = got_inputs.reshape(-1, model_width)
    expert_grad = got_grad.reshape(-1, hidden_width)
    weight_gate = gate_weight[0]
    weight_up = up_weight[0]
    local_hidden = weight_gate.shape[1]
    column_start = shard_index * local_hidden
    input_rows = lax.all_gather(expert_inputs, "sq", axis=0, tiled=True)
    grad_rows = lax.all_gather(expert_grad, "sq", axis=0, tiled=True)
    cotangent = lax.dynamic_slice_in_dim(grad_rows, column_start, local_hidden, 1)
    summed = gate_term(input_rows, cotangent, weight_gate, weight_up)
    return lax.psum_scatter(
        summed[None].astype(jnp.bfloat16), "grp", scatter_dimension=1, tiled=True
    ).astype(jnp.float32)


def solution(mesh):
    return jax.shard_map(
        body,
        mesh=mesh,
        in_specs=(
            P(("grp", "ep", "sq"), None),
            P(("grp", "ep", "sq"), None),
            P(("grp", "ep", "sq"), None),
            P(),
            P(("grp", "ep", "sq"), None),
            P(("grp", "ep", "sq"), None),
            P(("grp", "ep", "sq"), None),
            P("ep", None, "sq"),
            P("ep", None, "sq"),
        ),
        out_specs=P("ep", "grp", "sq"),
        check_vma=False,
    )
```

profile of v0, /device:TPU:0, one launch (start us, length us, event | category | flops | bytes accessed | tf_op | source)
XLA Modules:
  0.0 312.1 jit_solution(6690040816627483020)
XLA Ops:
  6.5 0.0 copy-start
  6.5 0.0 all-gather.3.cloned.1.call-start
  6.5 0.8 broadcast_multiply_fusion
  7.4 0.8 copy.15
  8.2 0.1 eq.46
  8.3 0.1 eq.42
  8.5 0.1 copy.14
  8.6 0.1 mul.78
  8.8 1.2 reduce-window.6
  10.0 0.2 slice_reduce_fusion
  10.2 0.2 reduce-window.9
  10.4 0.1 add_bitcast_fusion
  10.5 1.1 copy.17
  11.6 10.0 %all_gather.12 = bf16[512,512]{0,1:T(8,128)(2,1)} all-gather(bf16[256,512]{0,1:T(8,128)(2,1)S(1)} %copy.17), channel_id=1, replica_groups=mesh['grp'=4,'ep'=4,'sq'=2] {'sq'}, dimensions={0}, use_global_device_ids=true | all-gather | bytes 786432 | tf_op jit(solution)/shard_map/all_gather | solution.py:40
  21.7 8.4 %all_gather.13 = bf16[512,512]{1,0:T(8,128)(2,1)S(1)} all-gather(bf16[256,512]{1,0:T(8,128)(2,1)} %param.11), channel_id=1, replica_groups=mesh['grp'=4,'ep'=4,'sq'=2] {'sq'}, dimensions={0}, use_global_device_ids=true | all-gather | bytes 786432 | tf_op jit(solution)/shard_map/all_gather | solution.py:41
  30.0 1.0 copy.20
  31.0 1.8 reshape.173
  32.8 0.2 fusion.25
  33.0 2.7 fusion
  35.8 0.0 copy-start.2
  35.8 2.0 fusion.1
  37.8 0.0 copy-done.2
  37.8 0.0 copy-start.3
  37.8 2.5 multiply_reduce_fusion
  40.3 0.0 copy-done.3
  40.3 1.3 fusion.13
  41.7 1.5 copy.22
  43.1 2.6 broadcast_in_dim.51
  45.8 4.1 %reshape.185 = bf16[512,2048]{1,0:T(8,128)(2,1)} reshape(bf16[256,2,2048]{2,1,0:T(2,128)(2,1)} %broadcast_in_dim.51) | data formatting | bytes 4194304 | tf_op jit(solution)/shard_map/reshape | solution.py:74
  49.9 6.7 %scatter_custom_fusion = bf16[768,2048]{1,0:T(8,128)(2,1)} fusion(s32[512]{0:T(512)S(1)} %bitcast.79, bf16[512,2048]{1,0:T(8,128)(2,1)} %reshape.185, bf16[]{:T(256)} %constant.25.clone.1), kind=kCustom, calls=%fused_computation.23 | custom fusion | bytes 3146240 | tf_op jit(solution)/shard_map/scatter | solution.py:81
  56.6 74.8 %all_to_all.10 = bf16[4,192,2048]{2,1,0:T(8,128)(2,1)} all-to-all(bf16[4,192,2048]{2,1,0:T(8,128)(2,1)} %bitcast.72), channel_id=1, replica_groups=mesh['grp'=4,'ep'=4,'sq'=2] {'ep'}, dimensions={0} | all-to-all | bytes 6291456 | tf_op jit(solution)/shard_map/all_to_all | solution.py:89
  131.4 0.0 copy-start.4
  131.4 0.0 copy-start.1
  131.4 0.0 all-gather.3.cloned.1.call-update
  131.4 0.0 all-gather.5.cloned.1.call-start
  131.5 0.6 copy-done.4
  132.1 0.1 copy.23
  132.2 0.1 mul.89
  132.4 0.1 copy-done.1
  132.5 2.0 broadcast_in_dim.53
  134.4 3.7 %convert_element_type.40 = f32[512,1024]{1,0:T(8,128)} reshape(f32[256,2,1024]{2,1,0:T(2,128)} %broadcast_in_dim.53) | data formatting | bytes 4194304 | tf_op jit(solution)/shard_map/convert_element_type | solution.py:76
  138.1 5.3 %scatter_custom_fusion.1 = bf16[768,1024]{1,0:T(8,128)(2,1)} fusion(s32[512]{0:T(512)S(1)} %bitcast.80, f32[512,1024]{1,0:T(8,128)} %convert_element_type.40, f32[512]{0:T(512)S(1)} %mul.89, bf16[]{:T(256)} %constant.25.clone.1), kind=kCustom, calls=%fused_computation.25 | custom fusion | flops 1048576 | bytes 3672066 | tf_op jit(solution)/shard_map/scatter | solution.py:84
  143.4 40.3 %all_to_all.11 = bf16[4,192,1024]{2,1,0:T(8,128)(2,1)} all-to-all(bf16[4,192,1024]{2,1,0:T(8,128)(2,1)} %bitcast.74), channel_id=1, replica_groups=mesh['grp'=4,'ep'=4,'sq'=2] {'ep'}, dimensions={0} | all-to-all | bytes 3145728 | tf_op jit(solution)/shard_map/all_to_all | solution.py:90
  183.7 0.0 all-gather.5.cloned.1.call-update
  183.7 0.0 reduce-scatter.2.cloned.1.call-start
  183.7 26.9 %all-gather.3.cloned.1.call-done = bf16[1536,2048]{1,0:T(8,128)(2,1)} async-done(((bf16[768,2048]{1,0:T(8,128)(2,1)}), bf16[1536,2048]{1,0:T(8,128)(2,1)}) %all-gather.3.cloned.1.call-update) | async-done | bytes 6291472 | tf_op jit(solution)/shard_map/all_gather | solution.py:98
  210.7 8.5 %fusion.9 = f32[1536,512]{1,0:T(8,128)} fusion(bf16[1536,2048]{1,0:T(8,128)(2,1)} %all-gather.3.cloned.1.call-done, bf16[1,2048,512]{2,1,0:T(8,128)(2,1)} %param.16), kind=kOutput, calls=%fused_computation.14 | convolution fusion | flops 3221225472 | bytes 11534336 | tf_op jit(solution)/shard_map/dot_general | solution.py:17
  219.2 38.0 %all-gather.5.cloned.1.call-done = bf16[1536,1024]{1,0:T(8,128)(2,1)} async-done(((bf16[768,1024]{1,0:T(8,128)(2,1)}), bf16[1536,1024]{1,0:T(8,128)(2,1)}) %all-gather.5.cloned.1.call-update) | async-done | bytes 3145744 | tf_op jit(solution)/shard_map/all_gather | solution.py:99
  257.2 0.0 copy-done
  257.2 14.6 %fusion.8 = bf16[1,2048,512]{2,1,0:T(8,128)(2,1)} fusion(bf16[1536,2048]{1,0:T(8,128)(2,1)} %all-gather.3.cloned.1.call-done, f32[1536,512]{1,0:T(8,128)} %fusion.9, bf16[1,2048,512]{2,1,0:T(8,128)(2,1)S(1)} %copy-done, bf16[1536,1024]{1,0:T(8,128)(2,1)} %all-gather.5.cloned.1.call-done, s32[]{:T(128)S(6)} %select_n.44), kind=kOutput, calls=%fused_computation.13 | convolution fusion | flops 6452150272 | bytes 21495812 | tf_op jit(solution)/shard_map/dot_general | solution.py:22
  271.8 0.0 reduce-scatter.2.cloned.1.call-update
  271.8 31.6 %reduce-scatter.2.cloned.1.call-done = bf16[1,512,512]{2,1,0:T(8,128)(2,1)} async-done(((bf16[1,2048,512]{2,1,0:T(8,128)(2,1)}), bf16[1,512,512]{2,1,0:T(8,128)(2,1)}) %reduce-scatter.2.cloned.1.call-update) | async-done | bytes 524304 | tf_op jit(solution)/shard_map/reduce_scatter | solution.py:102
  303.4 2.1 convert_element_type.46
  (8 shorter events, 0.1 us)
Async XLA Ops:
  6.5 250.7 %copy-start = (bf16[1,2048,512]{2,1,0:T(8,128)(2,1)S(1)}, bf16[1,2048,512]{2,1,0:T(8,128)(2,1)}, u32[]{:S(2)}) copy-start(bf16[1,2048,512]{2,1,0:T(8,128)(2,1)} %param.17) | copy-start | bytes 6291460
  6.5 204.1 %all-gather.3.cloned.1.call-start = ((), (), s32[]{:S(2)}) async-start(), calls=%async_computation.3 | async-start | bytes 9437184 | tf_op jit(solution)/shard_map/all_gather | solution.py:98
  35.8 2.0 copy-start.2
  37.8 2.5 copy-start.3
  131.4 0.7 copy-start.4
  131.4 1.1 copy-start.1
  131.4 125.8 %all-gather.5.cloned.1.call-start = ((), (), s32[]{:S(2)}) async-start(), calls=%async_computation.4 | async-start | bytes 4718592 | tf_op jit(solution)/shard_map/all_gather | solution.py:99
  183.7 119.7 %reduce-scatter.2.cloned.1.call-start = ((), (), s32[]{:S(2)}) async-start(), calls=%async_computation.5 | async-start | bytes 2621440 | tf_op jit(solution)/shard_map/reduce_scatter | solution.py:102
Sparse Core Ops, SparseCore 0:
  131.6 79.0 all-gather.2
  212.2 44.9 all-gather.4
  272.0 31.4 reduce-scatter.1
where the time goes:
time: 313 us; the launch traced here: 312 us
  blocking collectives  133 us (42%)
  waiting for transfers between devices  96.5 us (31%)
  matrix products  28.4 us (9%)
  local copies, waits for them, and re-layouts  27 us (9%)
  other arithmetic  13.3 us (4%)
  between operations  13.3 us (4%)
    all_to_all x1, blocking collectives, body(): lax.all_to_all(send_inputs, 'ep', split_axis=0, concat_axis=0, tiled=True)  74.8 us
    all_to_all x1, blocking collectives, body(): lax.all_to_all(send_grad, 'ep', split_axis=0, concat_axis=0, tiled=True)  40.3 us
    all_gather x1, waiting for transfers between devices, body(): grad_rows = lax.all_gather(expert_grad, 'sq', axis=0, tiled=True)  38 us
    reduce_scatter x1, waiting for transfers between devices, body(): lax.psum_scatter(summed[None].astype(jnp.bfloat16), 'grp', scatter_dimens...  31.6 us
    all_gather x1, waiting for transfers between devices, body(): input_rows = lax.all_gather(expert_inputs, 'sq', axis=0, tiled=True)  26.9 us
    dot_general x1, matrix products, gate_term(): lax.dot_general(inputs, delta_gate, (((0,), (0,)), ((), ())), preferred_e...  14.6 us
    all_gather x1, blocking collectives, body(): key_rows = lax.all_gather(keys, 'sq', axis=0, tiled=True)  10 us
    dot_general x1, matrix products, gate_term(): pre_gate = jnp.dot(inputs, weight_gate, preferred_element_type=jnp.float32)  8.55 us
  transfers between devices with their start and end apart: 3, of which 3 were waited for; matrix products, arithmetic and copies ran while one was open for 6% of the time, Pallas kernels for 0%

commit v1 on v0

v1 whole, which is shorter than its diff:
```python
import functools
import math

import jax
import jax.numpy as jnp
from jax import lax
from jax.experimental import pallas as pl
from jax.experimental.pallas import tpu as pltpu
from jax.sharding import PartitionSpec as P

HEAD_DIM = 128

epsilon = 1e-05
masked_score = -1e30


def attention_kernel(group_size, shard_ref, q_ref, ko_ref, vo_ref, kp_ref, vp_ref, gain_ref, out_ref, acc_ref):
    rows, model_width = q_ref.shape
    past = kp_ref.shape[0]
    scale = 1.0 / math.sqrt(HEAD_DIM)
    shard = shard_ref[0]
    contract = (((1,), (1,)), ((), ()))
    causal = lax.broadcasted_iota(jnp.int32, (rows, rows), 1) <= lax.broadcasted_iota(
        jnp.int32, (rows, rows), 0
    )
    seen = lax.broadcasted_iota(jnp.int32, (rows, past), 1) < shard * rows
    squares = jnp.zeros((rows, 1), jnp.float32)
    for head in range(model_width // HEAD_DIM):
        cols = slice(head * HEAD_DIM, (head + 1) * HEAD_DIM)
        kv = head // group_size
        kv_cols = slice(kv * HEAD_DIM, (kv + 1) * HEAD_DIM)
        q = q_ref[:, cols]
        own = lax.dot_general(q, ko_ref[:, kv_cols], contract, preferred_element_type=jnp.float32)
        old = lax.dot_general(q, kp_ref[:, kv_cols], contract, preferred_element_type=jnp.float32)
        own = jnp.where(causal, own * scale, masked_score)
        old = jnp.where(seen, old * scale, masked_score)
        top = jnp.maximum(
            jnp.max(own, axis=1, keepdims=True), jnp.max(old, axis=1, keepdims=True)
        )
        own = jnp.exp(own - top)
        old = jnp.exp(old - top)
        total = jnp.sum(own, axis=1, keepdims=True) + jnp.sum(old, axis=1, keepdims=True)
        out = jnp.dot(
            own.astype(jnp.bfloat16), vo_ref[:, kv_cols], preferred_element_type=jnp.float32
        ) + jnp.dot(
            old.astype(jnp.bfloat16), vp_ref[:, kv_cols], preferred_element_type=jnp.float32
        )
        out = out / total
        acc_ref[:, cols] = out
        squares = squares + jnp.sum(out * out, axis=1, keepdims=True)
    inverse = lax.rsqrt(squares / model_width + epsilon)
    out_ref[...] = (acc_ref[...] * inverse * gain_ref[...]).astype(jnp.bfloat16)


def attend(shard, queries, keys, values, past_keys, past_values, norm_gain):
    rows, model_width = queries.shape
    group_size = model_width // keys.shape[1]
    vmem = pl.BlockSpec(memory_space=pltpu.VMEM)
    return pl.pallas_call(
        functools.partial(attention_kernel, group_size),
        out_shape=jax.ShapeDtypeStruct((rows, model_width), jnp.bfloat16),
        in_specs=[pl.BlockSpec(memory_space=pltpu.SMEM)] + [vmem] * 6,
        out_specs=vmem,
        scratch_shapes=[pltpu.VMEM((rows, model_width), jnp.float32)],
        compiler_params=pltpu.CompilerParams(vmem_limit_bytes=32 << 20),
        cost_estimate=pl.CostEstimate(
            flops=4 * rows * model_width * (rows + past_keys.shape[0]),
            bytes_accessed=4 * rows * model_width,
            transcendentals=rows * (model_width // HEAD_DIM) * (rows + past_keys.shape[0]),
        ),
    )(shard.reshape(1), queries, keys, values, past_keys, past_values, norm_gain.reshape(1, -1))


def ring(size, shift):
    return [(i, (i + shift) % size) for i in range(size)]


def body(
    queries, keys, values, norm_gain, expert_ids, gate_values, hidden_grad, gate_weight, up_weight
):
    rows, model_width = queries.shape
    n_ep = lax.axis_size("ep")
    n_sq = lax.axis_size("sq")
    shard = lax.axis_index("sq")
    expert = lax.axis_index("ep")
    weight_gate = gate_weight[0]
    weight_up = up_weight[0]
    width = weight_gate.shape[1]
    kv_width = keys.shape[1]

    both = jnp.concatenate([keys, values], axis=1)
    past = []
    for j in range(1, n_sq):
        past.append(lax.ppermute(both, "sq", [(i, i + j) for i in range(n_sq - j)]))
    past = jnp.concatenate(past, axis=0)

    def columns_of(owner):
        return lax.dynamic_slice_in_dim(hidden_grad, owner * width, width, 1)

    grads = [columns_of(shard)]
    for j in range(1, n_sq):
        grads.append(lax.ppermute(columns_of((shard + j) % n_sq), "sq", ring(n_sq, j)))
    grad = jnp.concatenate(grads, axis=0)

    chosen = expert_ids[:, :, None] == jnp.arange(n_ep, dtype=jnp.int32)
    share = jnp.sum(jnp.where(chosen, gate_values[:, :, None], 0.0), axis=1).T
    shares = lax.all_gather(share, ("ep", "sq"), axis=0, tiled=False)
    shares = lax.dynamic_index_in_dim(shares, expert, 1, keepdims=False).reshape(n_ep, n_sq, rows)
    order = (shard - jnp.arange(n_sq)) % n_sq
    shares = jnp.take(shares, order, axis=1).reshape(n_ep, n_sq * rows)

    normed = attend(
        shard, queries, keys, values, past[:, :kv_width], past[:, kv_width:], norm_gain
    )

    def add_chunk(step, tokens, grad, summed):
        source = (expert - step) % n_ep
        share_here = lax.dynamic_index_in_dim(shares, source, 0, keepdims=False)
        pieces = [tokens]
        for j in range(1, n_sq):
            pieces.append(lax.ppermute(tokens, "sq", ring(n_sq, j)))
        for j, inputs in enumerate(pieces):
            part = slice(j * rows, (j + 1) * rows)
            cotangent = (share_here[part, None] * grad[part].astype(jnp.float32)).astype(
                jnp.bfloat16
            )
            pre_gate = jnp.dot(inputs, weight_gate, preferred_element_type=jnp.float32)
            pre_up = jnp.dot(inputs, weight_up, preferred_element_type=jnp.float32)
            sigmoid_gate = jax.nn.sigmoid(pre_gate)
            slope = sigmoid_gate * (1.0 + pre_gate * (1.0 - sigmoid_gate))
            delta = (cotangent.astype(jnp.float32) * pre_up * slope).astype(jnp.bfloat16)
            term = lax.dot_general(
                inputs, delta, (((0,), (0,)), ((), ())), preferred_element_type=jnp.float32
            )
            summed = term if summed is None else summed + term
        return summed

    def turn(tokens, grad):
        return lax.ppermute(tokens, "ep", ring(n_ep, 1)), lax.ppermute(grad, "ep", ring(n_ep, 1))

    if n_ep <= 8:
        summed = None
        tokens = normed
        for step in range(n_ep):
            if step < n_ep - 1:
                turned = turn(tokens, grad)
            summed = add_chunk(step, tokens, grad, summed)
            if step < n_ep - 1:
                tokens, grad = turned
    else:

        def one_step(step, carried):
            tokens, grad, summed = carried
            turned = turn(tokens, grad)
            return (*turned, add_chunk(step, tokens, grad, summed))

        start = jnp.zeros((model_width, width), jnp.float32)
        summed = lax.fori_loop(0, n_ep, one_step, (normed, grad, start))[2]
    return lax.psum_scatter(
        summed[None].astype(jnp.bfloat16), "grp", scatter_dimension=1, tiled=True
    ).astype(jnp.float32)


def solution(mesh):
    return jax.shard_map(
        body,
        mesh=mesh,
        in_specs=(
            P(("grp", "ep", "sq"), None),
            P(("grp", "ep", "sq"), None),
            P(("grp", "ep", "sq"), None),
            P(),
            P(("grp", "ep", "sq"), None),
            P(("grp", "ep", "sq"), None),
            P(("grp", "ep", "sq"), None),
            P("ep", None, "sq"),
            P("ep", None, "sq"),
        ),
        out_specs=P("ep", "grp", "sq"),
        check_vma=False,
    )
```

time: 313 us -> 232 us (0.74)
  blocking collectives: 133 us -> 37.2 us
  matrix products: 28.4 us -> 70.9 us
  local copies, waits for them, and re-layouts: 27 us -> 5.51 us
  waiting for transfers between devices: 96.5 us -> 79.7 us
  starting transfers between devices: 0.09 us -> 14.7 us
  other arithmetic: 13.3 us -> 4.11 us
  Pallas kernels: 0 us -> 5.68 us
    all_to_all x2 -> x0, blocking collectives: 115 us -> none  [the longest x1 74.8 us: body(): lax.all_to_all(send_inputs, 'ep', split_axis=0, concat_axis=0, tiled=True)]
    all_gather x2 -> x0, waiting for transfers between devices: 64.9 us -> none  [the longest x1 38 us: body(): grad_rows = lax.all_gather(expert_grad, 'sq', axis=0, tiled=True)]
    ppermute x0 -> x12, waiting for transfers between devices: none -> 49.3 us  [the longest x3 27.2 us: turn(): lax.ppermute(grad, 'ep', ring(n_ep, 1))]
    dot_general x4 -> x16, matrix products: 28.4 us -> 70.9 us  [the longest x8 48.7 us: add_chunk(): lax.dot_general(inputs, delta, (((0,), (0,)), ((), ())), preferred_elemen...]
    all_gather x2 -> x1, blocking collectives: 18.4 us -> 37.2 us  [body(): shares = lax.all_gather(share, ('ep', 'sq'), axis=0, tiled=False)]
    ppermute x0 -> x12, starting transfers between devices: none -> 14.7 us  [the longest x4 8.05 us: add_chunk(): pieces.append(lax.ppermute(tokens, 'sq', ring(n_sq, j)))]
    scatter x1 -> x0, local copies, waits for them, and re-layouts: 6.71 us -> none  [body(): send_inputs = jnp.zeros((experts * capacity, model_width), jnp.bfloat16)....]
    reshape x2, local copies, waits for them, and re-layouts: 5.9 us -> 0.01 us  [body(): lax.dynamic_index_in_dim(shares, expert, 1, keepdims=False)]
  transfers between devices with their start and end apart: 3 -> 13, of which waited for: 3 -> 6; matrix products, arithmetic and copies ran while one was open for 6% -> 25% of each run, Pallas kernels for 0% -> 2%
where the time goes in v1:
time: 232 us
  waiting for transfers between devices  79.7 us (34%)
  matrix products  70.9 us (31%)
  blocking collectives  37.2 us (16%)
  starting transfers between devices  14.7 us (6%)
  between operations  13.7 us (6%)
  Pallas kernels  5.68 us (2%)
  local copies, waits for them, and re-layouts  5.51 us (2%)
  other arithmetic  4.11 us (2%)
    dot_general x8, matrix products, add_chunk(): lax.dot_general(inputs, delta, (((0,), (0,)), ((), ())), preferred_elemen...  48.7 us
    all_gather x1, blocking collectives, body(): shares = lax.all_gather(share, ('ep', 'sq'), axis=0, tiled=False)  37.2 us
    reduce_scatter x1, waiting for transfers between devices, body(): lax.psum_scatter(summed[None].astype(jnp.bfloat16), 'grp', scatter_dimens...  30.3 us
    ppermute x3, waiting for transfers between devices, turn(): lax.ppermute(grad, 'ep', ring(n_ep, 1))  27.2 us
    dot_general x8, matrix products, add_chunk(): pre_gate = jnp.dot(inputs, weight_gate, preferred_element_type=jnp.float32)  22.2 us
    ppermute x3, waiting for transfers between devices, turn(): lax.ppermute(tokens, 'ep', ring(n_ep, 1))  19.2 us
    ppermute x4, starting transfers between devices, add_chunk(): pieces.append(lax.ppermute(tokens, 'sq', ring(n_sq, j)))  8.05 us
    pallas_call x1, Pallas kernels, attend(): pl.pallas_call(functools.partial(attention_kernel, group_size), out_shape...  5.68 us
  transfers between devices with their start and end apart: 13, of which 6 were waited for; matrix products, arithmetic and copies ran while one was open for 25% of the time, Pallas kernels for 2%

profile of v1, /device:TPU:0, one launch (start us, length us, event | category | flops | bytes accessed | tf_op | source)
XLA Modules:
  0.0 231.6 jit_solution(14900521530428341671)
XLA Ops:
  6.5 0.0 copy-start
  6.5 0.0 reduce-scatter.2.cloned.1.call-start
  6.6 0.0 copy-start.1
  6.6 0.0 copy-start.4
  6.6 1.9 constant_dynamic-slice_fusion.5
  8.5 3.0 %collective-permute-start.2 = (bf16[256,512]{1,0:T(8,128)(2,1)}, bf16[256,512]{1,0:T(8,128)(2,1)S(1)}, u32[]{:S(2)}, u32[]{:S(2)}) collective-permute-start(bf16[256,512]{1,0:T(8,128)(2,1)} %get-tuple-element.6), channel_id=1, source_target_pairs={{0,1},{1,0},{2,3},{3,2},{4,5},{5,4},{6,7},{7,6},{8,9},{9,8},{10,11... | collective-permute-start | bytes 786440 | tf_op jit(solution)/shard_map/ppermute | solution.py:102
  11.5 1.9 pad_maximum_fusion
  13.4 2.0 collective-permute-start
  15.4 0.0 copy-done.10
  15.4 0.0 copy-done.11
  15.5 0.1 broadcast_in_dim.38
  15.6 37.2 %all-gather.1 = f32[8,4,256]{2,1,0:T(4,128)S(1)} all-gather(f32[1,4,256]{2,1,0:T(4,128)S(1)} %bitcast.128), channel_id=2, replica_groups=mesh['grp'=4,'ep'=4,'sq'=2] {'ep','sq'}, dimensions={0}, use_global_device_ids=true | all-gather | bytes 36864 | tf_op jit(solution)/shard_map/all_gather | solution.py:107
  52.9 0.6 gather_fusion
  53.5 0.0 collective-permute-done.2
  53.5 0.1 collective-permute-start.4
  53.6 0.0 collective-permute-done
  53.7 0.0 copy-done.5
  53.7 0.5 copy-done.7
  54.2 0.0 copy-done.1
  54.2 0.0 copy-done.4
  54.2 0.9 copy-done.2
  55.1 1.2 copy-done.3
  56.4 5.7 %shard_map.91 = bf16[256,2048]{1,0:T(8,128)(2,1)S(1)} custom-call(s32[1]{0:T(128)} %bitcast.shard_ref, bf16[256,2048]{1,0:T(8,128)(2,1)S(1)} %copy-done.3, bf16[256,512]{1,0:T(8,128)(2,1)S(1)} %copy-done.1, bf16[256,512]{1,0:T(8,128)(2,1)S(1)} %copy-done.2, bf16[256,512]{1,0:T(8,128)(2,1)S(1)} %get-tuple-element.8.kp_ref, ...), custom_call_target="tpu_custom_call" | custom-call | flops 1073741824 | bytes 2097152 | tf_op jit(solution)/shard_map/pallas_call | solution.py:59
  62.1 0.1 collective-permute-start.3
  62.2 0.1 fusion.170
  62.2 2.9 %collective-permute-start.1 = (bf16[256,2048]{1,0:T(8,128)(2,1)S(1)}, bf16[256,2048]{1,0:T(8,128)(2,1)}, u32[]{:S(2)}, u32[]{:S(2)}) collective-permute-start(bf16[256,2048]{1,0:T(8,128)(2,1)S(1)} %shard_map.91), channel_id=1, source_target_pairs={{0,1},{1,0},{2,3},{3,2},{4,5},{5,4},{6,7},{7,6},{8,9},{9,8},{10,11... | collective-permute-start | bytes 3145736 | tf_op jit(solution)/shard_map/ppermute | solution.py:121
  65.1 3.6 %collective-permute-done.4 = bf16[512,512]{1,0:T(8,128)(2,1)} collective-permute-done((bf16[512,512]{1,0:T(8,128)(2,1)S(1)}, bf16[512,512]{1,0:T(8,128)(2,1)}, u32[]{:S(2)}, u32[]{:S(2)}) %collective-permute-start.4) | collective-permute-done | bytes 524320 | tf_op jit(solution)/shard_map/ppermute | solution.py:139
  68.7 0.0 collective-permute-start.7
  68.7 1.5 fusion.15
  70.3 0.0 copy-done
  70.3 4.5 %fusion.70 = f32[2048,512]{1,0:T(8,128)} fusion(bf16[256,2048]{1,0:T(8,128)(2,1)S(1)} %shard_map.91, bf16[1,2048,512]{2,1,0:T(8,128)(2,1)S(1)} %copy-done, f32[256,512]{1,0:T(8,128)} %fusion.15, bf16[256,512]{1,0:T(8,128)(2,1)S(1)} %copy-done.6, f32[256]{0:T(256)S(1)} %bitcast.136), kind=kOutput, calls=%fused_computation.47 | convolution fusion | flops 1075576832 | bytes 8127488 | tf_op jit(solution)/shard_map/dot_general | solution.py:132
  74.7 23.6 %collective-permute-done.7 = bf16[512,512]{1,0:T(8,128)(2,1)} collective-permute-done((bf16[512,512]{1,0:T(8,128)(2,1)}, bf16[512,512]{1,0:T(8,128)(2,1)}, u32[]{:S(2)}, u32[]{:S(2)}) %collective-permute-start.7) | collective-permute-done | bytes 524320 | tf_op jit(solution)/shard_map/ppermute | solution.py:139
  98.4 0.0 collective-permute-start.10
  98.4 0.0 collective-permute-done.3
  98.4 2.2 collective-permute-start.5
  100.6 1.5 collective-permute-start.6
  102.2 3.4 %fusion.11 = f32[256,512]{1,0:T(8,128)} fusion(bf16[256,2048]{1,0:T(8,128)(2,1)} %collective-permute-done.3, bf16[1,2048,512]{2,1,0:T(8,128)(2,1)} %param.16), kind=kOutput, calls=%fused_computation.13 | convolution fusion | flops 536870912 | bytes 3670016 | tf_op jit(solution)/shard_map/dot_general | solution.py:127
  105.6 0.0 collective-permute-done.1
  105.6 2.0 fusion.13
  107.6 5.1 %fusion.121 = f32[2048,512]{1,0:T(8,128)} fusion(bf16[256,2048]{1,0:T(8,128)(2,1)} %collective-permute-done.3, f32[256,512]{1,0:T(8,128)S(1)} %copy-done.9, bf16[1,2048,512]{2,1,0:T(8,128)(2,1)S(1)} %copy-done, bf16[512,512]{1,0:T(8,128)(2,1)} %collective-permute-done.4, f32[256]{0:T(256)S(1)} %bitcast.135), kind=kOutput, calls=%fused_computation.101 | convolution fusion | flops 1075576832 | bytes 9176064 | tf_op jit(solution)/shard_map/dot_general | solution.py:132
  112.7 5.0 %fusion.116 = f32[2048,512]{1,0:T(8,128)} fusion(bf16[256,2048]{1,0:T(8,128)(2,1)} %collective-permute-done.1, f32[256,512]{1,0:T(8,128)S(1)} %fusion.13, bf16[256,512]{1,0:T(8,128)(2,1)S(1)} %copy-done.8, bf16[1,2048,512]{2,1,0:T(8,128)(2,1)S(1)} %copy-done, f32[256]{0:T(256)S(1)} %bitcast.134), kind=kOutput, calls=%fused_computation.100 | convolution fusion | flops 1075576832 | bytes 8127488 | tf_op jit(solution)/shard_map/dot_general | solution.py:132
  117.7 15.1 %collective-permute-done.6 = bf16[256,2048]{1,0:T(8,128)(2,1)} collective-permute-done((bf16[256,2048]{1,0:T(8,128)(2,1)}, bf16[256,2048]{1,0:T(8,128)(2,1)}, u32[]{:S(2)}, u32[]{:S(2)}) %collective-permute-start.6) | collective-permute-done | bytes 1048608 | tf_op jit(solution)/shard_map/ppermute | solution.py:139
  132.9 2.1 collective-permute-start.8
  135.0 0.0 collective-permute-start.9
  135.0 3.4 %fusion.7 = f32[256,512]{1,0:T(8,128)} fusion(bf16[256,2048]{1,0:T(8,128)(2,1)} %collective-permute-done.6, bf16[1,2048,512]{2,1,0:T(8,128)(2,1)} %param.16), kind=kOutput, calls=%fused_computation.9 | convolution fusion | flops 536870912 | bytes 3670016 | tf_op jit(solution)/shard_map/dot_general | solution.py:127
  138.4 5.2 %fusion.126 = f32[2048,512]{1,0:T(8,128)} fusion(bf16[256,2048]{1,0:T(8,128)(2,1)} %collective-permute-done.6, f32[256,512]{1,0:T(8,128)} %fusion.7, bf16[1,2048,512]{2,1,0:T(8,128)(2,1)S(1)} %copy-done, bf16[512,512]{1,0:T(8,128)(2,1)} %collective-permute-done.7, f32[256]{0:T(256)S(1)} %bitcast.133), kind=kOutput, calls=%fused_computation.102 | convolution fusion | flops 1075576832 | bytes 9176064 | tf_op jit(solution)/shard_map/dot_general | solution.py:132
  143.6 0.0 collective-permute-done.5
  143.6 3.4 %fusion.9 = f32[256,512]{1,0:T(8,128)} fusion(bf16[256,2048]{1,0:T(8,128)(2,1)} %collective-permute-done.5, bf16[1,2048,512]{2,1,0:T(8,128)(2,1)} %param.16), kind=kOutput, calls=%fused_computation.11 | convolution fusion | flops 536870912 | bytes 3670016 | tf_op jit(solution)/shard_map/dot_general | solution.py:127
  147.0 5.3 %fusion.73 = f32[2048,512]{1,0:T(8,128)} fusion(bf16[256,2048]{1,0:T(8,128)(2,1)} %collective-permute-done.5, bf16[1,2048,512]{2,1,0:T(8,128)(2,1)S(1)} %copy-done, f32[256,512]{1,0:T(8,128)} %fusion.9, bf16[512,512]{1,0:T(8,128)(2,1)} %collective-permute-done.4, f32[256]{0:T(256)S(1)} %bitcast.132), kind=kOutput, calls=%fused_computation.48 | convolution fusion | flops 1075576832 | bytes 9176064 | tf_op jit(solution)/shard_map/dot_general | solution.py:132
  152.3 4.1 %collective-permute-done.9 = bf16[256,2048]{1,0:T(8,128)(2,1)S(1)} collective-permute-done((bf16[256,2048]{1,0:T(8,128)(2,1)}, bf16[256,2048]{1,0:T(8,128)(2,1)S(1)}, u32[]{:S(2)}, u32[]{:S(2)}) %collective-permute-start.9) | collective-permute-done | bytes 1048608 | tf_op jit(solution)/shard_map/ppermute | solution.py:139
  156.4 0.8 collective-permute-start.11
  157.1 3.1 %fusion.3 = f32[256,512]{1,0:T(8,128)} fusion(bf16[256,2048]{1,0:T(8,128)(2,1)S(1)} %collective-permute-done.9, bf16[1,2048,512]{2,1,0:T(8,128)(2,1)} %param.16), kind=kOutput, calls=%fused_computation.5 | convolution fusion | flops 536870912 | bytes 3670016 | tf_op jit(solution)/shard_map/dot_general | solution.py:127
  160.2 0.0 collective-permute-done.8
  160.2 0.0 copy-done.14
  160.2 2.8 %fusion.5 = f32[256,512]{1,0:T(8,128)} fusion(bf16[256,2048]{1,0:T(8,128)(2,1)} %collective-permute-done.8, bf16[1,2048,512]{2,1,0:T(8,128)(2,1)S(1)} %copy-done.14), kind=kOutput, calls=%fused_computation.7 | convolution fusion | flops 536870912 | bytes 3670016 | tf_op jit(solution)/shard_map/dot_general | solution.py:127
  163.0 5.4 %fusion.76 = f32[2048,512]{1,0:T(8,128)} fusion(bf16[256,2048]{1,0:T(8,128)(2,1)} %collective-permute-done.8, bf16[1,2048,512]{2,1,0:T(8,128)(2,1)S(1)} %copy-done, f32[256,512]{1,0:T(8,128)} %fusion.5, bf16[512,512]{1,0:T(8,128)(2,1)} %collective-permute-done.7, f32[256]{0:T(256)S(1)} %bitcast.131), kind=kOutput, calls=%fused_computation.49 | convolution fusion | flops 1075576832 | bytes 9176064 | tf_op jit(solution)/shard_map/dot_general | solution.py:132
  168.4 0.0 collective-permute-done.10
  168.4 4.6 %fusion.131 = f32[2048,512]{1,0:T(8,128)} fusion(bf16[256,2048]{1,0:T(8,128)(2,1)S(1)} %collective-permute-done.9, f32[256,512]{1,0:T(8,128)} %fusion.3, bf16[1,2048,512]{2,1,0:T(8,128)(2,1)S(1)} %copy-done, bf16[512,512]{1,0:T(8,128)(2,1)} %collective-permute-done.10, f32[256]{0:T(256)S(1)} %bitcast.130), kind=kOutput, calls=%fused_computation.103 | convolution fusion | flops 1075576832 | bytes 9176064 | tf_op jit(solution)/shard_map/dot_general | solution.py:132
  173.0 2.9 %collective-permute-done.11 = bf16[256,2048]{1,0:T(8,128)(2,1)} collective-permute-done((bf16[256,2048]{1,0:T(8,128)(2,1)S(1)}, bf16[256,2048]{1,0:T(8,128)(2,1)}, u32[]{:S(2)}, u32[]{:S(2)}) %collective-permute-start.11) | collective-permute-done | bytes 1048608 | tf_op jit(solution)/shard_map/ppermute | solution.py:121
  175.9 2.6 %fusion.1 = f32[256,512]{1,0:T(8,128)S(1)} fusion(bf16[256,2048]{1,0:T(8,128)(2,1)} %collective-permute-done.11, bf16[1,2048,512]{2,1,0:T(8,128)(2,1)} %param.16), kind=kOutput, calls=%fused_computation.3 | convolution fusion | flops 536870912 | bytes 3670016 | tf_op jit(solution)/shard_map/dot_general | solution.py:127
  178.5 13.7 %fusion = bf16[1,2048,512]{2,1,0:T(8,128)(2,1)} fusion(bf16[256,2048]{1,0:T(8,128)(2,1)} %collective-permute-done.11, f32[2048,512]{1,0:T(8,128)} %fusion.131, f32[2048,512]{1,0:T(8,128)} %fusion.76, f32[2048,512]{1,0:T(8,128)} %fusion.126, f32[2048,512]{1,0:T(8,128)} %fusion.73, f32[2048,512]{1,0:T(8,128)} %fusion.121, f32[2048,512]{1,0:T(8,128)} %fusion.70, ...), kind=kOutput, calls=%fused_computation.2 | convolution fusion | flops 1083965440 | bytes 36439040 | tf_op jit(solution)/shard_map/dot_general | solution.py:132
  192.2 0.0 reduce-scatter.2.cloned.1.call-update
  192.2 30.3 %reduce-scatter.2.cloned.1.call-done = bf16[1,512,512]{2,1,0:T(8,128)(2,1)} async-done(((bf16[1,2048,512]{2,1,0:T(8,128)(2,1)}), bf16[1,512,512]{2,1,0:T(8,128)(2,1)}) %reduce-scatter.2.cloned.1.call-update) | async-done | bytes 524304 | tf_op jit(solution)/shard_map/reduce_scatter | solution.py:159
  222.6 2.1 convert_element_type.139
  (28 shorter events, 0.2 us)
Async XLA Ops:
  6.5 63.7 %copy-start = (bf16[1,2048,512]{2,1,0:T(8,128)(2,1)S(1)}, bf16[1,2048,512]{2,1,0:T(8,128)(2,1)}, u32[]{:S(2)}) copy-start(bf16[1,2048,512]{2,1,0:T(8,128)(2,1)} %param.17) | copy-start | bytes 6291460
  6.5 8.9 %copy-start.10 = (f32[256,2]{0,1:T(2,128)S(1)}, f32[256,2]{0,1:T(2,128)}, u32[]{:S(2)}) copy-start(f32[256,2]{0,1:T(2,128)} %param.14) | copy-start | bytes 6148
  6.5 8.9 %copy-start.11 = (s32[256,2]{0,1:T(2,128)S(1)}, s32[256,2]{0,1:T(2,128)}, u32[]{:S(2)}) copy-start(s32[256,2]{0,1:T(2,128)} %param.13) | copy-start | bytes 6148
  6.5 216.0 %reduce-scatter.2.cloned.1.call-start = ((), (), s32[]{:S(2)}) async-start(), calls=%async_computation.1 | async-start | bytes 2621440 | tf_op jit(solution)/shard_map/reduce_scatter | solution.py:159
  6.6 47.6 %copy-start.1 = (bf16[256,512]{1,0:T(8,128)(2,1)S(1)}, bf16[256,512]{1,0:T(8,128)(2,1)}, u32[]{:S(2)}) copy-start(bf16[256,512]{1,0:T(8,128)(2,1)} %ko_ref.1) | copy-start | bytes 786436
  6.6 47.6 %copy-start.4 = (f32[2048]{0:T(1024)S(1)}, f32[2048]{0:T(1024)}, u32[]{:S(2)}) copy-start(f32[2048]{0:T(1024)} %param.12) | copy-start | bytes 24580
  8.5 45.1 %copy-start.5 = (bf16[256,512]{1,0:T(8,128)(2,1)}, bf16[256,512]{1,0:T(8,128)(2,1)S(1)}, u32[]{:S(2)}) copy-start(bf16[256,512]{1,0:T(8,128)(2,1)S(1)} %get-tuple-element.5) | copy-start | bytes 786436
  8.5 45.0 %collective-permute-start.2 = (bf16[256,512]{1,0:T(8,128)(2,1)}, bf16[256,512]{1,0:T(8,128)(2,1)S(1)}, u32[]{:S(2)}, u32[]{:S(2)}) collective-permute-start(bf16[256,512]{1,0:T(8,128)(2,1)} %get-tuple-element.6), channel_id=1, source_target_pairs={{0,1},{1,0},{2,3},{3,2},{4,5},{5,4},{6,7},{7,6},{8,9},{9,8},{10,11... | collective-permute-start | bytes 786440 | tf_op jit(solution)/shard_map/ppermute | solution.py:102
  13.4 40.2 %collective-permute-start = (bf16[256,1024]{1,0:T(8,128)(2,1)}, bf16[256,1024]{1,0:T(8,128)(2,1)S(1)}, u32[]{:S(2)}, u32[]{:S(2)}) collective-permute-start(bf16[256,1024]{1,0:T(8,128)(2,1)} %pad_maximum_fusion), channel_id=1, source_target_pairs={{0,1},{2,3},{4,5},{6,7},{8,9},{10,11},{12,13},{14,15},{16,17},{18,... | collective-permute-start | bytes 1572872 | tf_op jit(solution)/shard_map/ppermute | solution.py:94
  53.5 0.7 copy-start.7
  53.5 15.2 %collective-permute-start.4 = (bf16[512,512]{1,0:T(8,128)(2,1)S(1)}, bf16[512,512]{1,0:T(8,128)(2,1)}, u32[]{:S(2)}, u32[]{:S(2)}) collective-permute-start(bf16[512,512]{1,0:T(8,128)(2,1)S(1)} %pad_maximum_fusion.1), channel_id=1, source_target_pairs={{0,2},{2,4},{4,6},{6,0},{1,3},{3,5},{5,7},{7,1},{8,10},{10,12},{12... | collective-permute-start | bytes 1572872 | tf_op jit(solution)/shard_map/ppermute | solution.py:139
  54.2 1.0 copy-start.2
  55.1 1.2 copy-start.3
  56.4 12.4 %copy-start.12 = (bf16[1,2048,512]{2,1,0:T(8,128)(2,1)S(1)}, bf16[1,2048,512]{2,1,0:T(8,128)(2,1)}, u32[]{:S(2)}) copy-start(bf16[1,2048,512]{2,1,0:T(8,128)(2,1)} %param.16) | copy-start | bytes 6291460
  62.1 8.2 %copy-start.6 = (bf16[256,512]{1,0:T(8,128)(2,1)S(1)}, bf16[256,512]{1,0:T(8,128)(2,1)}, u32[]{:S(2)}) copy-start(bf16[256,512]{1,0:T(8,128)(2,1)} %copy-done.5) | copy-start | bytes 786436
  62.1 36.3 %collective-permute-start.3 = (bf16[256,2048]{1,0:T(8,128)(2,1)S(1)}, bf16[256,2048]{1,0:T(8,128)(2,1)}, u32[]{:S(2)}, u32[]{:S(2)}) collective-permute-start(bf16[256,2048]{1,0:T(8,128)(2,1)S(1)} %shard_map.91), channel_id=1, source_target_pairs={{0,2},{2,4},{4,6},{6,0},{1,3},{3,5},{5,7},{7,1},{8,10},{10,12},{12... | collective-permute-start | bytes 3145736 | tf_op jit(solution)/shard_map/ppermute | solution.py:139
  62.2 43.3 %collective-permute-start.1 = (bf16[256,2048]{1,0:T(8,128)(2,1)S(1)}, bf16[256,2048]{1,0:T(8,128)(2,1)}, u32[]{:S(2)}, u32[]{:S(2)}) collective-permute-start(bf16[256,2048]{1,0:T(8,128)(2,1)S(1)} %shard_map.91), channel_id=1, source_target_pairs={{0,1},{1,0},{2,3},{3,2},{4,5},{5,4},{6,7},{7,6},{8,9},{9,8},{10,11... | collective-permute-start | bytes 3145736 | tf_op jit(solution)/shard_map/ppermute | solution.py:121
  68.7 29.7 %collective-permute-start.7 = (bf16[512,512]{1,0:T(8,128)(2,1)}, bf16[512,512]{1,0:T(8,128)(2,1)}, u32[]{:S(2)}, u32[]{:S(2)}) collective-permute-start(bf16[512,512]{1,0:T(8,128)(2,1)} %collective-permute-done.4), channel_id=1, source_target_pairs={{0,2},{2,4},{4,6},{6,0},{1,3},{3,5},{5,7},{7,1},{8,10},{10,12},{12... | collective-permute-start | bytes 1572872 | tf_op jit(solution)/shard_map/ppermute | solution.py:139
  74.7 30.9 %copy-start.13 = (bf16[1,2048,512]{2,1,0:T(8,128)(2,1)S(1)}, bf16[1,2048,512]{2,1,0:T(8,128)(2,1)}, u32[]{:S(2)}) copy-start(bf16[1,2048,512]{2,1,0:T(8,128)(2,1)} %param.16) | copy-start | bytes 6291460
  98.4 70.0 %collective-permute-start.10 = (bf16[512,512]{1,0:T(8,128)(2,1)}, bf16[512,512]{1,0:T(8,128)(2,1)}, u32[]{:S(2)}, u32[]{:S(2)}) collective-permute-start(bf16[512,512]{1,0:T(8,128)(2,1)} %collective-permute-done.7), channel_id=1, source_target_pairs={{0,2},{2,4},{4,6},{6,0},{1,3},{3,5},{5,7},{7,1},{8,10},{10,12},{12... | collective-permute-start | bytes 1572872 | tf_op jit(solution)/shard_map/ppermute | solution.py:139
  98.4 45.2 %collective-permute-start.5 = (bf16[256,2048]{1,0:T(8,128)(2,1)}, bf16[256,2048]{1,0:T(8,128)(2,1)}, u32[]{:S(2)}, u32[]{:S(2)}) collective-permute-start(bf16[256,2048]{1,0:T(8,128)(2,1)} %collective-permute-done.3), channel_id=1, source_target_pairs={{0,1},{1,0},{2,3},{3,2},{4,5},{5,4},{6,7},{7,6},{8,9},{9,8},{10,11... | collective-permute-start | bytes 3145736 | tf_op jit(solution)/shard_map/ppermute | solution.py:121
  100.6 32.2 %collective-permute-start.6 = (bf16[256,2048]{1,0:T(8,128)(2,1)}, bf16[256,2048]{1,0:T(8,128)(2,1)}, u32[]{:S(2)}, u32[]{:S(2)}) collective-permute-start(bf16[256,2048]{1,0:T(8,128)(2,1)} %collective-permute-done.3), channel_id=1, source_target_pairs={{0,2},{2,4},{4,6},{6,0},{1,3},{3,5},{5,7},{7,1},{8,10},{10,12},{12... | collective-permute-start | bytes 3145736 | tf_op jit(solution)/shard_map/ppermute | solution.py:139
  105.6 2.0 copy-start.9
  107.6 5.1 %copy-start.8 = (bf16[256,512]{1,0:T(8,128)(2,1)S(1)}, bf16[256,512]{1,0:T(8,128)(2,1)}, u32[]{:S(2)}) copy-start(bf16[256,512]{1,0:T(8,128)(2,1)} %copy-done.7) | copy-start | bytes 786436
  132.9 27.4 %collective-permute-start.8 = (bf16[256,2048]{1,0:T(8,128)(2,1)}, bf16[256,2048]{1,0:T(8,128)(2,1)}, u32[]{:S(2)}, u32[]{:S(2)}) collective-permute-start(bf16[256,2048]{1,0:T(8,128)(2,1)} %collective-permute-done.6), channel_id=1, source_target_pairs={{0,1},{1,0},{2,3},{3,2},{4,5},{5,4},{6,7},{7,6},{8,9},{9,8},{10,11... | collective-permute-start | bytes 3145736 | tf_op jit(solution)/shard_map/ppermute | solution.py:121
  135.0 21.4 %collective-permute-start.9 = (bf16[256,2048]{1,0:T(8,128)(2,1)}, bf16[256,2048]{1,0:T(8,128)(2,1)S(1)}, u32[]{:S(2)}, u32[]{:S(2)}) collective-permute-start(bf16[256,2048]{1,0:T(8,128)(2,1)} %collective-permute-done.6), channel_id=1, source_target_pairs={{0,2},{2,4},{4,6},{6,0},{1,3},{3,5},{5,7},{7,1},{8,10},{10,12},{12... | collective-permute-start | bytes 3145736 | tf_op jit(solution)/shard_map/ppermute | solution.py:139
  152.3 7.9 %copy-start.14 = (bf16[1,2048,512]{2,1,0:T(8,128)(2,1)S(1)}, bf16[1,2048,512]{2,1,0:T(8,128)(2,1)}, u32[]{:S(2)}) copy-start(bf16[1,2048,512]{2,1,0:T(8,128)(2,1)} %param.16) | copy-start | bytes 6291460
  156.4 19.5 %collective-permute-start.11 = (bf16[256,2048]{1,0:T(8,128)(2,1)S(1)}, bf16[256,2048]{1,0:T(8,128)(2,1)}, u32[]{:S(2)}, u32[]{:S(2)}) collective-permute-start(bf16[256,2048]{1,0:T(8,128)(2,1)S(1)} %collective-permute-done.9), channel_id=1, source_target_pairs={{0,1},{1,0},{2,3},{3,2},{4,5},{5,4},{6,7},{7,6},{8,9},{9,8},{10,11... | collective-permute-start | bytes 3145736 | tf_op jit(solution)/shard_map/ppermute | solution.py:121
Sparse Core Ops, SparseCore 0:
  192.3 30.1 reduce-scatter.1

commit v2 on v1

--- a/solution.py
+++ b/solution.py
@@ -12,6 +12,7 @@
 
 epsilon = 1e-05
 masked_score = -1e30
+MESH = pl.DeviceIdType.MESH
 
 
 def attention_kernel(group_size, shard_ref, q_ref, ko_ref, vo_ref, kp_ref, vp_ref, gain_ref, out_ref, acc_ref):
@@ -161,9 +162,287 @@
     ).astype(jnp.float32)
 
 
+def whole_kernel(
+    q_ref, k_ref, v_ref, gain_ref, share_ref, hidden_ref, gate_hbm, up_hbm, out_ref,
+    x_buf, g_buf, c_buf, kv_buf, weight_gate, weight_up, delta_ref, attended, acc,
+    stage, from_core, carry, from_chip,
+    load_sem, kv_send, kv_recv, yg_send, yg_recv, zg_send, zg_recv, zc_send, zc_recv,
+    zx_send, zx_recv, yx_send, yx_recv, core_send, core_recv, chip_send, chip_recv,
+):
+    n_ep = x_buf.shape[0]
+    rows, model_width = q_ref.shape
+    width = weight_gate.shape[1]
+    kv_heads = k_ref.shape[1] // HEAD_DIM
+    group_size = model_width // k_ref.shape[1]
+    half = rows // 2
+    block = model_width // 4
+    scale = 1.0 / math.sqrt(HEAD_DIM)
+    grp, expert, shard = lax.axis_index("grp"), lax.axis_index("ep"), lax.axis_index("sq")
+    peer = 1 - shard
+    right, left = lax.rem(expert + 1, n_ep), lax.rem(expert + n_ep - 1, n_ep)
+    core = lax.rem(grp, 2)
+    chip = grp // 2
+    sibling = chip * 2 + 1 - core
+    across = (1 - chip) * 2 + core
+    diagonal = (1 - chip) * 2 + 1 - core
+
+    loads = [
+        pltpu.make_async_copy(gate_hbm, weight_gate, load_sem.at[0]),
+        pltpu.make_async_copy(up_hbm, weight_up, load_sem.at[1]),
+    ]
+    for load in loads:
+        load.start()
+
+    barrier = pltpu.get_barrier_semaphore()
+    for target in ({"sq": peer}, {"ep": right}, {"ep": left}, {"grp": sibling}, {"grp": across}):
+        pl.semaphore_signal(barrier, inc=1, device_id=target, device_id_type=MESH)
+    pl.semaphore_wait(barrier, 5)
+
+    def send(src, dst, send_sem, recv_sem, target):
+        return pltpu.make_async_remote_copy(
+            src_ref=src, dst_ref=dst, send_sem=send_sem, recv_sem=recv_sem,
+            device_id=target, device_id_type=MESH,
+        )
+
+    def part(h):
+        return pl.ds(pl.multiple_of(h * half, half), half)
+
+    def zx(s, h):
+        return send(x_buf.at[s, 0, part(h)], x_buf.at[s + 1, 0, part(h)],
+                    zx_send.at[s, h], zx_recv.at[s, h], {"ep": right})
+
+    def yx(s, h):
+        return send(x_buf.at[s, 0, part(h)], x_buf.at[s, 1, part(h)],
+                    yx_send.at[s, h], yx_recv.at[s, h], {"sq": peer})
+
+    def zg(s, j):
+        return send(g_buf.at[s, j], g_buf.at[s + 1, j],
+                    zg_send.at[s, j], zg_recv.at[s, j], {"ep": right})
+
+    def zc(s, j):
+        return send(c_buf.at[s, j], c_buf.at[s + 1, j],
+                    zc_send.at[s, j], zc_recv.at[s, j], {"ep": right})
+
+    y_keys = send(k_ref, kv_buf.at[0], kv_send.at[0], kv_recv.at[0], {"sq": peer})
+    y_values = send(v_ref, kv_buf.at[1], kv_send.at[1], kv_recv.at[1], {"sq": peer})
+    peer_columns = pl.ds(pl.multiple_of(peer * width, width), width)
+    own_columns = pl.ds(pl.multiple_of(shard * width, width), width)
+    y_grad = send(hidden_ref.at[:, peer_columns], g_buf.at[0, 1],
+                  yg_send.at[0], yg_recv.at[0], {"sq": peer})
+    y_share = send(share_ref, c_buf.at[0, 1], yg_send.at[1], yg_recv.at[1], {"sq": peer})
+    y_keys.start()
+    y_values.start()
+    y_share.start()
+    y_grad.start()
+    g_buf[0, 0] = hidden_ref[:, own_columns]
+    c_buf[0, 0] = share_ref[...]
+    zc(0, 0).start()
+    zg(0, 0).start()
+    acc[...] = jnp.zeros_like(acc)
+    y_keys.wait_recv()
+    y_values.wait_recv()
+
+    contract = (((1,), (1,)), ((), ()))
+
+    @pl.loop(0, 2)
+    def _(h):
+        causal = lax.broadcasted_iota(jnp.int32, (half, rows), 1) <= (
+            lax.broadcasted_iota(jnp.int32, (half, rows), 0) + h * half
+        )
+        seen = lax.broadcasted_iota(jnp.int32, (half, rows), 1) < shard * rows
+        squares = jnp.zeros((half, 1), jnp.float32)
+        for head in range(kv_heads * group_size):
+            cols = slice(head * HEAD_DIM, (head + 1) * HEAD_DIM)
+            kv = head // group_size
+            kv_cols = slice(kv * HEAD_DIM, (kv + 1) * HEAD_DIM)
+            q = q_ref[part(h), cols]
+            own = lax.dot_general(
+                q, k_ref[:, kv_cols], contract, preferred_element_type=jnp.float32
+            )
+            old = lax.dot_general(
+                q, kv_buf[0, :, kv_cols], contract, preferred_element_type=jnp.float32
+            )
+            own = jnp.where(causal, own * scale, masked_score)
+            old = jnp.where(seen, old * scale, masked_score)
+            top = jnp.maximum(
+                jnp.max(own, axis=1, keepdims=True), jnp.max(old, axis=1, keepdims=True)
+            )
+            own = jnp.exp(own - top)
+            old = jnp.exp(old - top)
+            total = jnp.sum(own, axis=1, keepdims=True) + jnp.sum(old, axis=1, keepdims=True)
+            out = jnp.dot(
+                own.astype(jnp.bfloat16), v_ref[:, kv_cols], preferred_element_type=jnp.float32
+            ) + jnp.dot(
+                old.astype(jnp.bfloat16), kv_buf[1, :, kv_cols],
+                preferred_element_type=jnp.float32,
+            )
+            out = out / total
+            attended[:, cols] = out
+            squares = squares + jnp.sum(out * out, axis=1, keepdims=True)
+        inverse = lax.rsqrt(squares / model_width + epsilon)
+        x_buf[0, 0, part(h)] = (attended[...] * inverse * gain_ref[...]).astype(jnp.bfloat16)
+        zx(0, h).start()
+        yx(0, h).start()
+
+    y_share.wait_recv()
+    y_grad.wait_recv()
+    zc(0, 1).start()
+    zg(0, 1).start()
+    for load in loads:
+        load.wait()
+
+    tile = min(256, width)
+
+    def deltas(s, j):
+        share = c_buf[s, j]
+        picked = lax.broadcasted_iota(jnp.int32, share.shape, 0) == expert
+        share = jnp.sum(jnp.where(picked, share, 0.0), axis=0, keepdims=True)
+        share = jnp.broadcast_to(share, (128, rows)).T[:, :1]
+
+        @pl.loop(0, width // tile)
+        def _(t):
+            cols = pl.ds(pl.multiple_of(t * tile, tile), tile)
+            inputs = x_buf[s, j]
+            pre_gate = jnp.dot(inputs, weight_gate[:, cols], preferred_element_type=jnp.float32)
+            pre_up = jnp.dot(inputs, weight_up[:, cols], preferred_element_type=jnp.float32)
+            cotangent = (share * g_buf[s, j, :, cols].astype(jnp.float32)).astype(jnp.bfloat16)
+            sigmoid_gate = 1.0 / (1.0 + jnp.exp(-pre_gate))
+            slope = sigmoid_gate * (1.0 + pre_gate * (1.0 - sigmoid_gate))
+            delta_ref[:, cols] = (cotangent.astype(jnp.float32) * pre_up * slope).astype(
+                jnp.bfloat16
+            )
+
+    def columns(b):
+        return pl.ds(pl.multiple_of(b * block, block), block)
+
+    def add_block(s, j, b):
+        return acc[:, columns(b)] + lax.dot_general(
+            delta_ref[...], x_buf[s, j, :, columns(b)], (((0,), (0,)), ((), ())),
+            preferred_element_type=jnp.float32,
+        )
+
+    def add_piece(s, j):
+        deltas(s, j)
+
+        @pl.loop(0, 4)
+        def _(b):
+            acc[:, columns(b)] = add_block(s, j, b)
+
+    @pl.loop(1, n_ep)
+    def _(s):
+        for j in range(2):
+            zc(s - 1, j).wait_recv()
+            zg(s - 1, j).wait_recv()
+
+            @pl.when(s < n_ep - 1)
+            def _():
+                zc(s, j).start()
+                zg(s, j).start()
+
+            zx(s - 1, j).wait_recv()
+
+            @pl.when(s < n_ep - 1)
+            def _():
+                zx(s, j).start()
+
+            yx(s, j).start()
+            if j == 1:
+                yx(s - 1, 0).wait_recv()
+                yx(s - 1, 1).wait_recv()
+            add_piece(s - 1, j)
+
+    last = n_ep - 1
+    add_piece(last, 0)
+    yx(last, 0).wait_recv()
+    yx(last, 1).wait_recv()
+    deltas(last, 1)
+
+    def to_core(i):
+        return send(stage.at[i], from_core.at[i], core_send.at[i], core_recv.at[i],
+                    {"grp": sibling})
+
+    to_chip = send(carry, from_chip, chip_send, chip_recv, {"grp": across})
+    stage[0] = add_block(last, 1, diagonal).astype(jnp.bfloat16)
+    to_core(0).start()
+    mine = add_block(last, 1, across)
+    to_core(0).wait_recv()
+    carry[...] = (mine + from_core[0].astype(jnp.float32)).astype(jnp.bfloat16)
+    to_chip.start()
+    stage[1] = add_block(last, 1, sibling).astype(jnp.bfloat16)
+    to_core(1).start()
+    acc[:, columns(grp)] = add_block(last, 1, grp)
+    to_core(1).wait_recv()
+    acc[:, columns(grp)] += from_core[1].astype(jnp.float32)
+    to_chip.wait_recv()
+    out_ref[...] = (acc[:, columns(grp)] + from_chip[...].astype(jnp.float32)).T
+
+    for copy in (y_keys, y_values, y_share, y_grad, to_core(0), to_core(1), to_chip):
+        copy.wait_send()
+
+    @pl.loop(0, n_ep)
+    def _(s):
+        for j in range(2):
+            yx(s, j).wait_send()
+
+            @pl.when(s < n_ep - 1)
+            def _():
+                zx(s, j).wait_send()
+                zg(s, j).wait_send()
+                zc(s, j).wait_send()
+
+
+def fused(
+    queries, keys, values, norm_gain, expert_ids, gate_values, hidden_grad, gate_weight, up_weight
+):
+    rows, model_width = queries.shape
+    n_ep = lax.axis_size("ep")
+    width = gate_weight.shape[2]
+    kv_width = keys.shape[1]
+    block = model_width // 4
+    chosen = expert_ids.T[:, None, :] == jnp.arange(8, dtype=jnp.int32)[:, None]
+    share = jnp.sum(jnp.where(chosen, gate_values.T[:, None, :], 0.0), axis=0)
+    vmem = pl.BlockSpec(memory_space=pltpu.VMEM)
+    hbm = pl.BlockSpec(memory_space=pl.ANY)
+    dma = pltpu.SemaphoreType.DMA
+    bf16, f32 = jnp.bfloat16, jnp.float32
+    out = pl.pallas_call(
+        whole_kernel,
+        out_shape=jax.ShapeDtypeStruct((block, width), f32),
+        in_specs=[vmem] * 6 + [hbm] * 2,
+        out_specs=vmem,
+        scratch_shapes=[
+            pltpu.VMEM((n_ep, 2, rows, model_width), bf16),
+            pltpu.VMEM((n_ep, 2, rows, width), bf16),
+            pltpu.VMEM((n_ep, 2, 8, rows), f32),
+            pltpu.VMEM((2, rows, kv_width), bf16),
+            pltpu.VMEM((model_width, width), bf16),
+            pltpu.VMEM((model_width, width), bf16),
+            pltpu.VMEM((rows, width), bf16),
+            pltpu.VMEM((rows // 2, model_width), f32),
+            pltpu.VMEM((width, model_width), f32),
+            pltpu.VMEM((2, width, block), bf16),
+            pltpu.VMEM((2, width, block), bf16),
+            pltpu.VMEM((width, block), bf16),
+            pltpu.VMEM((width, block), bf16),
+            dma((2,)), dma((2,)), dma((2,)), dma((2,)), dma((2,)),
+            dma((n_ep, 2)), dma((n_ep, 2)), dma((n_ep, 2)), dma((n_ep, 2)),
+            dma((n_ep, 2)), dma((n_ep, 2)), dma((n_ep, 2)), dma((n_ep, 2)),
+            dma((2,)), dma((2,)), dma, dma,
+        ],
+        compiler_params=pltpu.CompilerParams(
+            collective_id=0, has_side_effects=True, vmem_limit_bytes=48 << 20
+        ),
+    )(
+        queries, keys, values, norm_gain.reshape(1, -1), share, hidden_grad,
+        gate_weight[0], up_weight[0],
+    )
+    return out[None]
+
+
 def solution(mesh):
+    small = mesh.shape["grp"] == 4 and mesh.shape["sq"] == 2 and 3 <= mesh.shape["ep"] <= 8
     return jax.shard_map(
-        body,
+        fused if small else body,
         mesh=mesh,
         in_specs=(
             P(("grp", "ep", "sq"), None),

time: 232 us -> 157 us (0.68)
  Pallas kernels: 5.68 us -> 148 us
  waiting for transfers between devices: 79.7 us -> 0 us
  matrix products: 70.9 us -> 0 us
  blocking collectives: 37.2 us -> 0 us
  starting transfers between devices: 14.7 us -> 0 us
  between operations: 13.7 us -> 0.02 us
  other arithmetic: 4.11 us -> 0.7 us
    pallas_call x1, Pallas kernels: 5.68 us -> 148 us  [fused(): pl.pallas_call(whole_kernel, out_shape=jax.ShapeDtypeStruct((block, width...]
    dot_general x16 -> x0, matrix products: 70.9 us -> none  [the longest x8 48.7 us: add_chunk(): lax.dot_general(inputs, delta, (((0,), (0,)), ((), ())), preferred_elemen...]
    ppermute x12 -> x0, waiting for transfers between devices: 49.3 us -> none  [the longest x3 27.2 us: turn(): lax.ppermute(grad, 'ep', ring(n_ep, 1))]
    all_gather x1 -> x0, blocking collectives: 37.2 us -> none  [body(): shares = lax.all_gather(share, ('ep', 'sq'), axis=0, tiled=False)]
    reduce_scatter x1 -> x0, waiting for transfers between devices: 30.3 us -> none  [body(): lax.psum_scatter(summed[None].astype(jnp.bfloat16), 'grp', scatter_dimens...]
    ppermute x12 -> x0, starting transfers between devices: 14.7 us -> none  [the longest x4 8.05 us: add_chunk(): pieces.append(lax.ppermute(tokens, 'sq', ring(n_sq, j)))]
    unnamed x30 -> x13, local copies, waits for them, and re-layouts: 2.74 us -> 7.42 us
  transfers between devices with their start and end apart: 13 -> 0, of which waited for: 6 -> 0; matrix products, arithmetic and copies ran while one was open for 25% -> 0% of each run, Pallas kernels for 2% -> 0%
where the time goes in v2:
time: 157 us; the launch traced here: 156 us
  Pallas kernels  148 us (94%)
  local copies, waits for them, and re-layouts  7.42 us (5%)
    pallas_call x1, Pallas kernels, fused(): pl.pallas_call(whole_kernel, out_shape=jax.ShapeDtypeStruct((block, width...  148 us
    unnamed x13, local copies, waits for them, and re-layouts  7.42 us

profile of v2, /device:TPU:0, one launch (start us, length us, event | category | flops | bytes accessed | tf_op | source)
XLA Modules:
  0.0 156.3 jit_solution(8507134434230981721)
XLA Ops:
  0.0 0.7 select_reduce_fusion.share_ref
  0.7 0.0 copy-start
  0.7 1.6 %copy-done = bf16[1,2048,512]{2,1,0:T(8,128)(2,1)S(1)} copy-done((bf16[1,2048,512]{2,1,0:T(8,128)(2,1)S(1)}, bf16[1,2048,512]{2,1,0:T(8,128)(2,1)}, u32[]{:S(2)}) %copy-start) | copy-done | bytes 2097176
  2.3 0.0 copy-start.1
  2.3 1.2 copy-done.1
  3.5 0.0 copy-start.2
  3.5 1.0 copy-done.2
  4.6 0.0 copy-start.3
  4.6 0.9 copy-done.3
  5.5 0.0 copy-start.4
  5.5 0.9 copy-done.4
  6.5 0.0 copy-start.5
  6.5 0.7 copy-done.5
  7.2 148.2 %shard_map.91 = f32[512,512]{1,0:T(8,128)S(1)} custom-call(bf16[256,2048]{1,0:T(8,128)(2,1)S(1)} %copy-done.1, bf16[256,512]{1,0:T(8,128)(2,1)S(1)} %copy-done.3, bf16[256,512]{1,0:T(8,128)(2,1)S(1)} %copy-done.4, f32[1,2048]{1,0:T(1,128)S(1)} %bitcast.8, f32[8,256]{1,0:T(8,128)S(1)} %select_reduce_fusion.share_ref, bf16[256,1024]{1,0:T(8,128)(2,1)S(1)} %copy-done.2, ...), custom_call_target="tpu_custom_call" | custom-call | tf_op jit(solution)/shard_map/pallas_call | solution.py:408
  155.4 1.0 copy.11
Async XLA Ops:
  0.7 1.6 %copy-start = (bf16[1,2048,512]{2,1,0:T(8,128)(2,1)S(1)}, bf16[1,2048,512]{2,1,0:T(8,128)(2,1)}, u32[]{:S(2)}) copy-start(bf16[1,2048,512]{2,1,0:T(8,128)(2,1)} %param.16) | copy-start | bytes 6291460
  2.3 1.2 copy-start.1
  3.5 1.0 copy-start.2
  4.6 0.9 copy-start.3
  5.5 0.9 copy-start.4
  6.5 0.7 copy-start.5

commit v3 on v2

--- a/solution.py
+++ b/solution.py
@@ -163,35 +163,47 @@
 
 
 def whole_kernel(
-    q_ref, k_ref, v_ref, gain_ref, share_ref, hidden_ref, gate_hbm, up_hbm, out_ref,
-    x_buf, g_buf, c_buf, kv_buf, weight_gate, weight_up, delta_ref, attended, acc,
-    stage, from_core, carry, from_chip,
-    load_sem, kv_send, kv_recv, yg_send, yg_recv, zg_send, zg_recv, zc_send, zc_recv,
-    zx_send, zx_recv, yx_send, yx_recv, core_send, core_recv, chip_send, chip_recv,
+    q_hbm, k_hbm, v_hbm, gain_ref, share_ref, hidden_hbm, gate_hbm, up_hbm, out_ref,
+    q_ref, k_ref, v_ref, x_full, x_comp, x_out, g_full, g_comp, g_out, c_buf, kv_buf,
+    weight_gate, weight_up, delta_ref, attended, acc, stage, from_core, carry, from_chip,
+    load_sem, y_send, y_recv, c_send, c_recv, g_send, g_recv, x_send, x_recv, yx_send, yx_recv,
+    core_send, core_recv, chip_send, chip_recv,
 ):
-    n_ep = x_buf.shape[0]
+    n_ep = x_full.shape[0]
     rows, model_width = q_ref.shape
+    cap = x_comp.shape[3]
+    half = model_width // 2
     width = weight_gate.shape[1]
     kv_heads = k_ref.shape[1] // HEAD_DIM
     group_size = model_width // k_ref.shape[1]
-    half = rows // 2
     block = model_width // 4
     scale = 1.0 / math.sqrt(HEAD_DIM)
     grp, expert, shard = lax.axis_index("grp"), lax.axis_index("ep"), lax.axis_index("sq")
     peer = 1 - shard
-    right, left = lax.rem(expert + 1, n_ep), lax.rem(expert + n_ep - 1, n_ep)
+    last = n_ep - 1
+    right, left = lax.rem(expert + 1, n_ep), lax.rem(expert + last, n_ep)
+    inner = jnp.logical_and(expert > 0, expert < last)
     core = lax.rem(grp, 2)
     chip = grp // 2
     sibling = chip * 2 + 1 - core
     across = (1 - chip) * 2 + core
     diagonal = (1 - chip) * 2 + 1 - core
+    peer_columns = pl.ds(pl.multiple_of(peer * width, width), width)
+    own_columns = pl.ds(pl.multiple_of(shard * width, width), width)
+
+    def load(i, src, dst):
+        return pltpu.make_async_copy(src, dst, load_sem.at[i])
 
     loads = [
-        pltpu.make_async_copy(gate_hbm, weight_gate, load_sem.at[0]),
-        pltpu.make_async_copy(up_hbm, weight_up, load_sem.at[1]),
+        load(0, q_hbm, q_ref),
+        load(1, k_hbm, k_ref),
+        load(2, v_hbm, v_ref),
+        load(3, hidden_hbm.at[:, own_columns], g_full.at[expert, 0]),
+        load(4, gate_hbm, weight_gate),
+        load(5, up_hbm, weight_up),
     ]
-    for load in loads:
-        load.start()
+    for copy in loads:
+        copy.start()
 
     barrier = pltpu.get_barrier_semaphore()
     for target in ({"sq": peer}, {"ep": right}, {"ep": left}, {"grp": sibling}, {"grp": across}):
@@ -204,58 +216,132 @@
             device_id=target, device_id_type=MESH,
         )
 
-    def part(h):
-        return pl.ds(pl.multiple_of(h * half, half), half)
-
-    def zx(s, h):
-        return send(x_buf.at[s, 0, part(h)], x_buf.at[s + 1, 0, part(h)],
-                    zx_send.at[s, h], zx_recv.at[s, h], {"ep": right})
-
-    def yx(s, h):
-        return send(x_buf.at[s, 0, part(h)], x_buf.at[s, 1, part(h)],
-                    yx_send.at[s, h], yx_recv.at[s, h], {"sq": peer})
-
-    def zg(s, j):
-        return send(g_buf.at[s, j], g_buf.at[s + 1, j],
-                    zg_send.at[s, j], zg_recv.at[s, j], {"ep": right})
-
-    def zc(s, j):
-        return send(c_buf.at[s, j], c_buf.at[s + 1, j],
-                    zc_send.at[s, j], zc_recv.at[s, j], {"ep": right})
-
-    y_keys = send(k_ref, kv_buf.at[0], kv_send.at[0], kv_recv.at[0], {"sq": peer})
-    y_values = send(v_ref, kv_buf.at[1], kv_send.at[1], kv_recv.at[1], {"sq": peer})
-    peer_columns = pl.ds(pl.multiple_of(peer * width, width), width)
-    own_columns = pl.ds(pl.multiple_of(shard * width, width), width)
-    y_grad = send(hidden_ref.at[:, peer_columns], g_buf.at[0, 1],
-                  yg_send.at[0], yg_recv.at[0], {"sq": peer})
-    y_share = send(share_ref, c_buf.at[0, 1], yg_send.at[1], yg_recv.at[1], {"sq": peer})
+    def neighbour(d):
+        return {"ep": right if d else left}
+
+    def c_copy(z, j, d):
+        return send(c_buf.at[z, j], c_buf.at[z, j], c_send.at[d, z, j], c_recv.at[z, j],
+                    neighbour(d))
+
+    def g_whole(z, j, d):
+        return send(g_full.at[z, j], g_full.at[z, j], g_send.at[d, z, j], g_recv.at[z, j],
+                    neighbour(d))
+
+    def g_picked(z, j, d):
+        return send(g_out.at[z, j], g_comp.at[z, j], g_send.at[d, z, j], g_recv.at[z, j],
+                    neighbour(d))
+
+    def x_whole(z, h, d):
+        return send(x_full.at[z, h], x_full.at[z, h], x_send.at[d, z, h], x_recv.at[z, h],
+                    neighbour(d))
+
+    def x_picked(z, h, d):
+        return send(x_out.at[z, h], x_comp.at[z, 0, h], x_send.at[d, z, h], x_recv.at[z, h],
+                    neighbour(d))
+
+    def yx(z, h):
+        return send(x_comp.at[z, 0, h], x_comp.at[z, 1, h], yx_send.at[z, h], yx_recv.at[z, h],
+                    {"sq": peer})
+
+    def goes(d):
+        return expert < last if d else expert > 0
+
+    def to_inner(d):
+        return expert < last - 1 if d else expert > 1
+
+    def to_end(d):
+        return expert == last - 1 if d else expert == 1
+
+    def end_of(d):
+        return last if d else 0
+
+    y_keys = send(k_hbm, kv_buf.at[0], y_send.at[0], y_recv.at[0], {"sq": peer})
+    y_values = send(v_hbm, kv_buf.at[1], y_send.at[1], y_recv.at[1], {"sq": peer})
+    y_share = send(share_ref, c_buf.at[expert, 1], y_send.at[2], y_recv.at[2], {"sq": peer})
+    y_grad = send(hidden_hbm.at[:, peer_columns], g_full.at[expert, 1],
+                  y_send.at[3], y_recv.at[3], {"sq": peer})
+    y_share.start()
     y_keys.start()
     y_values.start()
-    y_share.start()
     y_grad.start()
-    g_buf[0, 0] = hidden_ref[:, own_columns]
-    c_buf[0, 0] = share_ref[...]
-    zc(0, 0).start()
-    zg(0, 0).start()
+    c_buf[expert, 0] = share_ref[...]
     acc[...] = jnp.zeros_like(acc)
+    upper = (
+        lax.broadcasted_iota(jnp.int32, (rows, rows), 0)
+        <= lax.broadcasted_iota(jnp.int32, (rows, rows), 1)
+    ).astype(jnp.float32).astype(jnp.bfloat16)
+    places = lax.broadcasted_iota(jnp.int32, (cap, rows), 0).astype(jnp.float32)
+
+    def pick(z, j, who):
+        share = c_buf[z, j]
+        here = lax.broadcasted_iota(jnp.int32, share.shape, 0) == who
+        share = jnp.sum(jnp.where(here, share, 0.0), axis=0, keepdims=True)
+        routed = jnp.where(share > 0.0, 1.0, 0.0)
+        count = jnp.dot(
+            jnp.broadcast_to(routed, (16, rows)).astype(jnp.bfloat16), upper,
+            preferred_element_type=jnp.float32,
+        )[:1]
+        key = jnp.where(share > 0.0, count - 1.0, -1.0)
+        return places == key, share
+
+    def chooser(z, j, who):
+        return jnp.where(pick(z, j, who)[0], 1.0, 0.0).astype(jnp.bfloat16)
+
+    def picked(choice, array):
+        return jnp.dot(choice, array, preferred_element_type=jnp.float32).astype(jnp.bfloat16)
+
+    def pass_grad(z, j, d):
+        @pl.when(goes(d))
+        def _():
+            c_copy(z, j, d).start()
+
+        @pl.when(to_inner(d))
+        def _():
+            g_whole(z, j, d).start()
+
+        @pl.when(to_end(d))
+        def _():
+            g_out[z, j] = picked(chooser(z, j, end_of(d)), g_full[z, j])
+            g_picked(z, j, d).start()
+
+    def pass_tokens(z, h, d):
+        @pl.when(to_inner(d))
+        def _():
+            x_whole(z, h, d).start()
+
+        @pl.when(to_end(d))
+        def _():
+            x_out[z, h] = picked(chooser(z, 0, end_of(d)), x_full[z, h])
+            x_picked(z, h, d).start()
+
+    def keep_tokens(z, h):
+        x_comp[z, 0, h] = picked(chooser(z, 0, expert), x_full[z, h])
+        yx(z, h).start()
+
+    loads[3].wait()
+    for d in range(2):
+        pass_grad(expert, 0, d)
+    for copy in loads[:3]:
+        copy.wait()
     y_keys.wait_recv()
     y_values.wait_recv()
 
     contract = (((1,), (1,)), ((), ()))
+    part_rows = rows // 2
 
     @pl.loop(0, 2)
-    def _(h):
-        causal = lax.broadcasted_iota(jnp.int32, (half, rows), 1) <= (
-            lax.broadcasted_iota(jnp.int32, (half, rows), 0) + h * half
+    def _(p):
+        part = pl.ds(pl.multiple_of(p * part_rows, part_rows), part_rows)
+        causal = lax.broadcasted_iota(jnp.int32, (part_rows, rows), 1) <= (
+            lax.broadcasted_iota(jnp.int32, (part_rows, rows), 0) + p * part_rows
         )
-        seen = lax.broadcasted_iota(jnp.int32, (half, rows), 1) < shard * rows
-        squares = jnp.zeros((half, 1), jnp.float32)
+        seen = lax.broadcasted_iota(jnp.int32, (part_rows, rows), 1) < shard * rows
+        squares = jnp.zeros((part_rows, 1), jnp.float32)
         for head in range(kv_heads * group_size):
             cols = slice(head * HEAD_DIM, (head + 1) * HEAD_DIM)
             kv = head // group_size
             kv_cols = slice(kv * HEAD_DIM, (kv + 1) * HEAD_DIM)
-            q = q_ref[part(h), cols]
+            q = q_ref[part, cols]
             own = lax.dot_general(
                 q, k_ref[:, kv_cols], contract, preferred_element_type=jnp.float32
             )
@@ -280,97 +366,128 @@
             attended[:, cols] = out
             squares = squares + jnp.sum(out * out, axis=1, keepdims=True)
         inverse = lax.rsqrt(squares / model_width + epsilon)
-        x_buf[0, 0, part(h)] = (attended[...] * inverse * gain_ref[...]).astype(jnp.bfloat16)
-        zx(0, h).start()
-        yx(0, h).start()
-
+        normed = (attended[...] * inverse * gain_ref[...]).astype(jnp.bfloat16)
+        x_full[expert, 0, part] = normed[:, :half]
+        x_full[expert, 1, part] = normed[:, half:]
+
+    for h in range(2):
+        for d in range(2):
+            pass_tokens(expert, h, d)
+        keep_tokens(expert, h)
     y_share.wait_recv()
     y_grad.wait_recv()
-    zc(0, 1).start()
-    zg(0, 1).start()
-    for load in loads:
-        load.wait()
+    for d in range(2):
+        pass_grad(expert, 1, d)
+    for j in range(2):
+        g_comp[expert, j] = picked(chooser(expert, j, expert), g_full[expert, j])
+    for copy in loads[4:]:
+        copy.wait()
 
     tile = min(256, width)
 
-    def deltas(s, j):
-        share = c_buf[s, j]
-        picked = lax.broadcasted_iota(jnp.int32, share.shape, 0) == expert
-        share = jnp.sum(jnp.where(picked, share, 0.0), axis=0, keepdims=True)
-        share = jnp.broadcast_to(share, (128, rows)).T[:, :1]
+    def columns(b):
+        return pl.ds(pl.multiple_of(b * block, block), block)
+
+    def add_piece(z, j):
+        where, share = pick(z, j, expert)
+        share = jnp.sum(jnp.where(where, share, 0.0), axis=1, keepdims=True)
 
         @pl.loop(0, width // tile)
         def _(t):
             cols = pl.ds(pl.multiple_of(t * tile, tile), tile)
-            inputs = x_buf[s, j]
-            pre_gate = jnp.dot(inputs, weight_gate[:, cols], preferred_element_type=jnp.float32)
-            pre_up = jnp.dot(inputs, weight_up[:, cols], preferred_element_type=jnp.float32)
-            cotangent = (share * g_buf[s, j, :, cols].astype(jnp.float32)).astype(jnp.bfloat16)
+
+            def product(weight):
+                return jnp.dot(
+                    x_comp[z, j, 0], weight[:half, cols], preferred_element_type=jnp.float32
+                ) + jnp.dot(
+                    x_comp[z, j, 1], weight[half:, cols], preferred_element_type=jnp.float32
+                )
+
+            pre_gate = product(weight_gate)
+            pre_up = product(weight_up)
+            cotangent = (share * g_comp[z, j, :, cols].astype(jnp.float32)).astype(jnp.bfloat16)
             sigmoid_gate = 1.0 / (1.0 + jnp.exp(-pre_gate))
             slope = sigmoid_gate * (1.0 + pre_gate * (1.0 - sigmoid_gate))
             delta_ref[:, cols] = (cotangent.astype(jnp.float32) * pre_up * slope).astype(
                 jnp.bfloat16
             )
 
-    def columns(b):
-        return pl.ds(pl.multiple_of(b * block, block), block)
-
-    def add_block(s, j, b):
-        return acc[:, columns(b)] + lax.dot_general(
-            delta_ref[...], x_buf[s, j, :, columns(b)], (((0,), (0,)), ((), ())),
-            preferred_element_type=jnp.float32,
-        )
-
-    def add_piece(s, j):
-        deltas(s, j)
-
-        @pl.loop(0, 4)
-        def _(b):
-            acc[:, columns(b)] = add_block(s, j, b)
-
-    @pl.loop(1, n_ep)
-    def _(s):
-        for j in range(2):
-            zc(s - 1, j).wait_recv()
-            zg(s - 1, j).wait_recv()
-
-            @pl.when(s < n_ep - 1)
+        for h in range(2):
+
+            @pl.loop(0, 2)
+            def _(b):
+                acc[:, columns(h * 2 + b)] += lax.dot_general(
+                    delta_ref[...], x_comp[z, j, h, :, columns(b)], (((0,), (0,)), ((), ())),
+                    preferred_element_type=jnp.float32,
+                )
+
+    def add_chunk(z):
+        @pl.loop(0, 2)
+        def _(j):
+            @pl.when(j == 1)
             def _():
-                zc(s, j).start()
-                zg(s, j).start()
-
-            zx(s - 1, j).wait_recv()
-
-            @pl.when(s < n_ep - 1)
+                yx(z, 0).wait_recv()
+                yx(z, 1).wait_recv()
+
+            add_piece(z, j)
+
+    def present(z):
+        return jnp.logical_and(z >= 0, z <= last)
+
+    @pl.loop(1, n_ep + 1)
+    def _(dist):
+        for d in range(2):
+            z = expert - dist if d else expert + dist
+
+            @pl.when(present(z))
             def _():
-                zx(s, j).start()
-
-            yx(s, j).start()
-            if j == 1:
-                yx(s - 1, 0).wait_recv()
-                yx(s - 1, 1).wait_recv()
-            add_piece(s - 1, j)
-
-    last = n_ep - 1
-    add_piece(last, 0)
-    yx(last, 0).wait_recv()
-    yx(last, 1).wait_recv()
-    deltas(last, 1)
+                for j in range(2):
+                    c_copy(z, j, d).wait_recv()
+
+            @pl.when(jnp.logical_and(present(z), inner))
+            def _():
+                for j in range(2):
+                    g_whole(z, j, d).wait_recv()
+                    pass_grad(z, j, d)
+                for h in range(2):
+                    x_whole(z, h, d).wait_recv()
+                    pass_tokens(z, h, d)
+                    keep_tokens(z, h)
+                for j in range(2):
+                    g_comp[z, j] = picked(chooser(z, j, expert), g_full[z, j])
+
+            @pl.when(jnp.logical_and(present(z), jnp.logical_not(inner)))
+            def _():
+                for j in range(2):
+                    g_picked(z, j, d).wait_recv()
+                for h in range(2):
+                    x_picked(z, h, d).wait_recv()
+                    yx(z, h).start()
+
+        @pl.when(dist == 1)
+        def _():
+            add_chunk(expert)
+
+        @pl.loop(0, 2)
+        def _(d):
+            z = expert + (dist - 1) * (1 - 2 * d)
+
+            @pl.when(jnp.logical_and(dist > 1, present(z)))
+            def _():
+                add_chunk(z)
 
     def to_core(i):
         return send(stage.at[i], from_core.at[i], core_send.at[i], core_recv.at[i],
                     {"grp": sibling})
 
     to_chip = send(carry, from_chip, chip_send, chip_recv, {"grp": across})
-    stage[0] = add_block(last, 1, diagonal).astype(jnp.bfloat16)
+    stage[0] = acc[:, columns(diagonal)].astype(jnp.bfloat16)
     to_core(0).start()
-    mine = add_block(last, 1, across)
+    stage[1] = acc[:, columns(sibling)].astype(jnp.bfloat16)
     to_core(0).wait_recv()
-    carry[...] = (mine + from_core[0].astype(jnp.float32)).astype(jnp.bfloat16)
+    carry[...] = (acc[:, columns(across)] + from_core[0].astype(jnp.float32)).astype(jnp.bfloat16)
     to_chip.start()
-    stage[1] = add_block(last, 1, sibling).astype(jnp.bfloat16)
     to_core(1).start()
-    acc[:, columns(grp)] = add_block(last, 1, grp)
     to_core(1).wait_recv()
     acc[:, columns(grp)] += from_core[1].astype(jnp.float32)
     to_chip.wait_recv()
@@ -380,15 +497,25 @@
         copy.wait_send()
 
     @pl.loop(0, n_ep)
-    def _(s):
-        for j in range(2):
-            yx(s, j).wait_send()
-
-            @pl.when(s < n_ep - 1)
-            def _():
-                zx(s, j).wait_send()
-                zg(s, j).wait_send()
-                zc(s, j).wait_send()
+    def _(z):
+        for i in range(2):
+            yx(z, i).wait_send()
+            for d in range(2):
+                passed = z <= expert if d else z >= expert
+
+                @pl.when(jnp.logical_and(passed, goes(d)))
+                def _():
+                    c_copy(z, i, d).wait_send()
+
+                @pl.when(jnp.logical_and(passed, to_inner(d)))
+                def _():
+                    g_whole(z, i, d).wait_send()
+                    x_whole(z, i, d).wait_send()
+
+                @pl.when(jnp.logical_and(passed, to_end(d)))
+                def _():
+                    g_picked(z, i, d).wait_send()
+                    x_picked(z, i, d).wait_send()
 
 
 def fused(
@@ -399,38 +526,47 @@
     width = gate_weight.shape[2]
     kv_width = keys.shape[1]
     block = model_width // 4
+    half = model_width // 2
+    cap = rows * expert_ids.shape[1] // n_ep * 3 // 2
     chosen = expert_ids.T[:, None, :] == jnp.arange(8, dtype=jnp.int32)[:, None]
     share = jnp.sum(jnp.where(chosen, gate_values.T[:, None, :], 0.0), axis=0)
     vmem = pl.BlockSpec(memory_space=pltpu.VMEM)
-    hbm = pl.BlockSpec(memory_space=pl.ANY)
+    hbm = pl.BlockSpec(memory_space=pltpu.HBM)
     dma = pltpu.SemaphoreType.DMA
     bf16, f32 = jnp.bfloat16, jnp.float32
     out = pl.pallas_call(
         whole_kernel,
         out_shape=jax.ShapeDtypeStruct((block, width), f32),
-        in_specs=[vmem] * 6 + [hbm] * 2,
+        in_specs=[hbm] * 3 + [vmem] * 2 + [hbm] * 3,
         out_specs=vmem,
         scratch_shapes=[
-            pltpu.VMEM((n_ep, 2, rows, model_width), bf16),
+            pltpu.VMEM((rows, model_width), bf16),
+            pltpu.VMEM((rows, kv_width), bf16),
+            pltpu.VMEM((rows, kv_width), bf16),
+            pltpu.VMEM((n_ep, 2, rows, half), bf16),
+            pltpu.VMEM((n_ep, 2, 2, cap, half), bf16),
+            pltpu.VMEM((n_ep, 2, cap, half), bf16),
             pltpu.VMEM((n_ep, 2, rows, width), bf16),
+            pltpu.VMEM((n_ep, 2, cap, width), bf16),
+            pltpu.VMEM((n_ep, 2, cap, width), bf16),
             pltpu.VMEM((n_ep, 2, 8, rows), f32),
             pltpu.VMEM((2, rows, kv_width), bf16),
             pltpu.VMEM((model_width, width), bf16),
             pltpu.VMEM((model_width, width), bf16),
-            pltpu.VMEM((rows, width), bf16),
+            pltpu.VMEM((cap, width), bf16),
             pltpu.VMEM((rows // 2, model_width), f32),
             pltpu.VMEM((width, model_width), f32),
             pltpu.VMEM((2, width, block), bf16),
             pltpu.VMEM((2, width, block), bf16),
             pltpu.VMEM((width, block), bf16),
             pltpu.VMEM((width, block), bf16),
-            dma((2,)), dma((2,)), dma((2,)), dma((2,)), dma((2,)),
-            dma((n_ep, 2)), dma((n_ep, 2)), dma((n_ep, 2)), dma((n_ep, 2)),
-            dma((n_ep, 2)), dma((n_ep, 2)), dma((n_ep, 2)), dma((n_ep, 2)),
+            dma((6,)), dma((4,)), dma((4,)),
+            dma((2, n_ep, 2)), dma((n_ep, 2)), dma((2, n_ep, 2)), dma((n_ep, 2)),
+            dma((2, n_ep, 2)), dma((n_ep, 2)), dma((n_ep, 2)), dma((n_ep, 2)),
             dma((2,)), dma((2,)), dma, dma,
         ],
         compiler_params=pltpu.CompilerParams(
-            collective_id=0, has_side_effects=True, vmem_limit_bytes=48 << 20
+            collective_id=0, has_side_effects=True, vmem_limit_bytes=56 << 20
         ),
     )(
         queries, keys, values, norm_gain.reshape(1, -1), share, hidden_grad,
@@ -440,7 +576,7 @@
 
 
 def solution(mesh):
-    small = mesh.shape["grp"] == 4 and mesh.shape["sq"] == 2 and 3 <= mesh.shape["ep"] <= 8
+    small = mesh.shape["grp"] == 4 and mesh.shape["sq"] == 2 and mesh.shape["ep"] == 4
     return jax.shard_map(
         fused if small else body,
         mesh=mesh,

time: 157 us -> 141 us (0.90)
  Pallas kernels: 148 us -> 135 us
  local copies, waits for them, and re-layouts: 7.42 us -> 2.26 us
    pallas_call x1, Pallas kernels: 148 us -> 135 us  [fused(): pl.pallas_call(whole_kernel, out_shape=jax.ShapeDtypeStruct((block, width...]
    unnamed x13 -> x1, local copies, waits for them, and re-layouts: 7.42 us -> 2.26 us
where the time goes in v3:
time: 141 us; the launch traced here: 139 us
  Pallas kernels  135 us (96%)
  local copies, waits for them, and re-layouts  2.26 us (2%)
    pallas_call x1, Pallas kernels, fused(): pl.pallas_call(whole_kernel, out_shape=jax.ShapeDtypeStruct((block, width...  135 us

profile of v3, /device:TPU:0, one launch (start us, length us, event | category | flops | bytes accessed | tf_op | source)
XLA Modules:
  0.0 139.0 jit_solution(8582612510025516995)
XLA Ops:
  0.0 1.3 select_reduce_fusion.share_ref
  1.3 135.5 %shard_map.91 = f32[512,512]{1,0:T(8,128)} custom-call(bf16[256,2048]{1,0:T(8,128)(2,1)} %q_hbm.1, bf16[256,512]{1,0:T(8,128)(2,1)} %k_hbm.1, bf16[256,512]{1,0:T(8,128)(2,1)} %v_hbm.1, f32[1,2048]{1,0:T(1,128)} %bitcast.9, f32[8,256]{1,0:T(8,128)} %select_reduce_fusion.share_ref, bf16[256,1024]{1,0:T(8,128)(2,1)} %hidden_hbm.1, bf16[2048,512]{1,0:T(8,128)(2,1)} %bitcast.7, ...), custom_call_target="tpu_custom_call" | custom-call | tf_op jit(solution)/shard_map/pallas_call | solution.py:537
  136.8 2.3 %copy.11 = f32[1,512,512]{2,1,0:T(8,128)} copy(f32[1,512,512]{2,1,0:T(8,128)} %bitcast.6) | data formatting | bytes 2097152

commit v4 on v3

--- a/solution.py
+++ b/solution.py
@@ -172,7 +172,8 @@
     n_ep = x_full.shape[0]
     rows, model_width = q_ref.shape
     cap = x_comp.shape[3]
-    half = model_width // 2
+    parts = x_full.shape[1]
+    half = model_width // parts
     width = weight_gate.shape[1]
     kv_heads = k_ref.shape[1] // HEAD_DIM
     group_size = model_width // k_ref.shape[1]
@@ -367,17 +368,20 @@
             squares = squares + jnp.sum(out * out, axis=1, keepdims=True)
         inverse = lax.rsqrt(squares / model_width + epsilon)
         normed = (attended[...] * inverse * gain_ref[...]).astype(jnp.bfloat16)
-        x_full[expert, 0, part] = normed[:, :half]
-        x_full[expert, 1, part] = normed[:, half:]
-
-    for h in range(2):
+        for h in range(parts):
+            x_full[expert, h, part] = normed[:, h * half : (h + 1) * half]
+
+        @pl.when(p == 0)
+        def _():
+            y_share.wait_recv()
+            y_grad.wait_recv()
+            for d in range(2):
+                pass_grad(expert, 1, d)
+
+    for h in range(parts):
         for d in range(2):
             pass_tokens(expert, h, d)
         keep_tokens(expert, h)
-    y_share.wait_recv()
-    y_grad.wait_recv()
-    for d in range(2):
-        pass_grad(expert, 1, d)
     for j in range(2):
         g_comp[expert, j] = picked(chooser(expert, j, expert), g_full[expert, j])
     for copy in loads[4:]:
@@ -397,10 +401,12 @@
             cols = pl.ds(pl.multiple_of(t * tile, tile), tile)
 
             def product(weight):
-                return jnp.dot(
-                    x_comp[z, j, 0], weight[:half, cols], preferred_element_type=jnp.float32
-                ) + jnp.dot(
-                    x_comp[z, j, 1], weight[half:, cols], preferred_element_type=jnp.float32
+                return sum(
+                    jnp.dot(
+                        x_comp[z, j, h], weight[h * half : (h + 1) * half, cols],
+                        preferred_element_type=jnp.float32,
+                    )
+                    for h in range(parts)
                 )
 
             pre_gate = product(weight_gate)
@@ -412,22 +418,20 @@
                 jnp.bfloat16
             )
 
-        for h in range(2):
-
-            @pl.loop(0, 2)
-            def _(b):
-                acc[:, columns(h * 2 + b)] += lax.dot_general(
-                    delta_ref[...], x_comp[z, j, h, :, columns(b)], (((0,), (0,)), ((), ())),
-                    preferred_element_type=jnp.float32,
-                )
+        @pl.loop(0, 4)
+        def _(b):
+            acc[:, columns(b)] += lax.dot_general(
+                delta_ref[...], x_comp[z, j, b], (((0,), (0,)), ((), ())),
+                preferred_element_type=jnp.float32,
+            )
 
     def add_chunk(z):
         @pl.loop(0, 2)
         def _(j):
             @pl.when(j == 1)
             def _():
-                yx(z, 0).wait_recv()
-                yx(z, 1).wait_recv()
+                for h in range(parts):
+                    yx(z, h).wait_recv()
 
             add_piece(z, j)
 
@@ -449,7 +453,7 @@
                 for j in range(2):
                     g_whole(z, j, d).wait_recv()
                     pass_grad(z, j, d)
-                for h in range(2):
+                for h in range(parts):
                     x_whole(z, h, d).wait_recv()
                     pass_tokens(z, h, d)
                     keep_tokens(z, h)
@@ -460,7 +464,7 @@
             def _():
                 for j in range(2):
                     g_picked(z, j, d).wait_recv()
-                for h in range(2):
+                for h in range(parts):
                     x_picked(z, h, d).wait_recv()
                     yx(z, h).start()
 
@@ -476,46 +480,77 @@
             def _():
                 add_chunk(z)
 
-    def to_core(i):
-        return send(stage.at[i], from_core.at[i], core_send.at[i], core_recv.at[i],
-                    {"grp": sibling})
-
-    to_chip = send(carry, from_chip, chip_send, chip_recv, {"grp": across})
-    stage[0] = acc[:, columns(diagonal)].astype(jnp.bfloat16)
-    to_core(0).start()
-    stage[1] = acc[:, columns(sibling)].astype(jnp.bfloat16)
-    to_core(0).wait_recv()
-    carry[...] = (acc[:, columns(across)] + from_core[0].astype(jnp.float32)).astype(jnp.bfloat16)
-    to_chip.start()
-    to_core(1).start()
-    to_core(1).wait_recv()
-    acc[:, columns(grp)] += from_core[1].astype(jnp.float32)
-    to_chip.wait_recv()
-    out_ref[...] = (acc[:, columns(grp)] + from_chip[...].astype(jnp.float32)).T
-
-    for copy in (y_keys, y_values, y_share, y_grad, to_core(0), to_core(1), to_chip):
+    slab = width // 2
+
+    def to_core(i, t):
+        rows_of = pl.ds(t * slab, slab)
+        return send(stage.at[i, rows_of], from_core.at[i, rows_of], core_send.at[i, t],
+                    core_recv.at[i, t], {"grp": sibling})
+
+    def to_chip(t):
+        rows_of = pl.ds(t * slab, slab)
+        return send(carry.at[rows_of], from_chip.at[rows_of], chip_send.at[t], chip_recv.at[t],
+                    {"grp": across})
+
+    slabs = [slice(0, slab), slice(slab, width)]
+    for t in range(2):
+        stage[0, slabs[t]] = acc[slabs[t], columns(diagonal)].astype(jnp.bfloat16)
+        to_core(0, t).start()
+    for t in range(2):
+        to_core(0, t).wait_recv()
+        carry[slabs[t]] = (
+            acc[slabs[t], columns(across)] + from_core[0, slabs[t]].astype(jnp.float32)
+        ).astype(jnp.bfloat16)
+        to_chip(t).start()
+    for t in range(2):
+        stage[1, slabs[t]] = acc[slabs[t], columns(sibling)].astype(jnp.bfloat16)
+        to_core(1, t).start()
+    for t in range(2):
+        to_core(1, t).wait_recv()
+        acc[slabs[t], columns(grp)] += from_core[1, slabs[t]].astype(jnp.float32)
+    for t in range(2):
+        to_chip(t).wait_recv()
+        out_ref[:, slabs[t]] = (
+            acc[slabs[t], columns(grp)] + from_chip[slabs[t]].astype(jnp.float32)
+        ).T
+
+    for copy in (y_keys, y_values, y_share, y_grad):
         copy.wait_send()
+    for t in range(2):
+        to_core(0, t).wait_send()
+        to_core(1, t).wait_send()
+        to_chip(t).wait_send()
 
     @pl.loop(0, n_ep)
     def _(z):
-        for i in range(2):
-            yx(z, i).wait_send()
+        for h in range(parts):
+            yx(z, h).wait_send()
             for d in range(2):
                 passed = z <= expert if d else z >= expert
 
+                @pl.when(jnp.logical_and(passed, to_inner(d)))
+                def _():
+                    x_whole(z, h, d).wait_send()
+
+                @pl.when(jnp.logical_and(passed, to_end(d)))
+                def _():
+                    x_picked(z, h, d).wait_send()
+
+        for j in range(2):
+            for d in range(2):
+                passed = z <= expert if d else z >= expert
+
                 @pl.when(jnp.logical_and(passed, goes(d)))
                 def _():
-                    c_copy(z, i, d).wait_send()
+                    c_copy(z, j, d).wait_send()
 
                 @pl.when(jnp.logical_and(passed, to_inner(d)))
                 def _():
-                    g_whole(z, i, d).wait_send()
-                    x_whole(z, i, d).wait_send()
+                    g_whole(z, j, d).wait_send()
 
                 @pl.when(jnp.logical_and(passed, to_end(d)))
                 def _():
-                    g_picked(z, i, d).wait_send()
-                    x_picked(z, i, d).wait_send()
+                    g_picked(z, j, d).wait_send()
 
 
 def fused(
@@ -526,7 +561,8 @@
     width = gate_weight.shape[2]
     kv_width = keys.shape[1]
     block = model_width // 4
-    half = model_width // 2
+    parts = 4
+    half = model_width // parts
     cap = rows * expert_ids.shape[1] // n_ep * 3 // 2
     chosen = expert_ids.T[:, None, :] == jnp.arange(8, dtype=jnp.int32)[:, None]
     share = jnp.sum(jnp.where(chosen, gate_values.T[:, None, :], 0.0), axis=0)
@@ -543,9 +579,9 @@
             pltpu.VMEM((rows, model_width), bf16),
             pltpu.VMEM((rows, kv_width), bf16),
             pltpu.VMEM((rows, kv_width), bf16),
-            pltpu.VMEM((n_ep, 2, rows, half), bf16),
-            pltpu.VMEM((n_ep, 2, 2, cap, half), bf16),
-            pltpu.VMEM((n_ep, 2, cap, half), bf16),
+            pltpu.VMEM((n_ep, parts, rows, half), bf16),
+            pltpu.VMEM((n_ep, 2, parts, cap, half), bf16),
+            pltpu.VMEM((n_ep, parts, cap, half), bf16),
             pltpu.VMEM((n_ep, 2, rows, width), bf16),
             pltpu.VMEM((n_ep, 2, cap, width), bf16),
             pltpu.VMEM((n_ep, 2, cap, width), bf16),
@@ -562,8 +598,8 @@
             pltpu.VMEM((width, block), bf16),
             dma((6,)), dma((4,)), dma((4,)),
             dma((2, n_ep, 2)), dma((n_ep, 2)), dma((2, n_ep, 2)), dma((n_ep, 2)),
-            dma((2, n_ep, 2)), dma((n_ep, 2)), dma((n_ep, 2)), dma((n_ep, 2)),
-            dma((2,)), dma((2,)), dma, dma,
+            dma((2, n_ep, parts)), dma((n_ep, parts)), dma((n_ep, parts)), dma((n_ep, parts)),
+            dma((2, 2)), dma((2, 2)), dma((2,)), dma((2,)),
         ],
         compiler_params=pltpu.CompilerParams(
             collective_id=0, has_side_effects=True, vmem_limit_bytes=56 << 20

time: 141 us -> 136 us (0.965)
  the two profiles are of different devices: /device:TPU:0 before, /device:TPU:25 now
where the time goes in v4:
time: 136 us
  Pallas kernels  132 us (97%)
  local copies, waits for them, and re-layouts  2.26 us (2%)
    pallas_call x1, Pallas kernels, fused(): pl.pallas_call(whole_kernel, out_shape=jax.ShapeDtypeStruct((block, width...  132 us

profile of v4, /device:TPU:25, one launch (start us, length us, event | category | flops | bytes accessed | tf_op | source)
XLA Modules:
  0.0 135.9 jit_solution(7037296918274345573)
XLA Ops:
  0.0 1.3 select_reduce_fusion.share_ref
  1.3 132.3 %shard_map.91 = f32[512,512]{1,0:T(8,128)} custom-call(bf16[256,2048]{1,0:T(8,128)(2,1)} %q_hbm.1, bf16[256,512]{1,0:T(8,128)(2,1)} %k_hbm.1, bf16[256,512]{1,0:T(8,128)(2,1)} %v_hbm.1, f32[1,2048]{1,0:T(1,128)} %bitcast.9, f32[8,256]{1,0:T(8,128)} %select_reduce_fusion.share_ref, bf16[256,1024]{1,0:T(8,128)(2,1)} %hidden_hbm.1, bf16[2048,512]{1,0:T(8,128)(2,1)} %bitcast.7, ...), custom_call_target="tpu_custom_call" | custom-call | tf_op jit(solution)/shard_map/pallas_call | solution.py:573
  133.6 2.3 %copy.11 = f32[1,512,512]{2,1,0:T(8,128)} copy(f32[1,512,512]{2,1,0:T(8,128)} %bitcast.6) | data formatting | bytes 2097152
